TPU v7x, 32 devices: a whole 2x2x4 slice. The times are simulated.
32 devices in a mesh: group: 4 (over y, x), tensor: 8 (over z, core).
Axes of the slice: x: 2, y: 2, z: 4, core: 2. Of those that a mesh axis runs over, the one named last changes fastest.
Arguments:
- prefill_states: bfloat16 [16384, 8192], P('group', 'tensor'), may hold values from -6 to 6
- key_weight: bfloat16 [8192, 1024], P('tensor'), may hold values from -0.0625 to 0.0625
- value_weight: bfloat16 [8192, 1024], P('tensor'), may hold values from -0.0625 to 0.0625
- page_slot: int32 [4, 8, 64], P('group', 'tensor'), may hold values from 0 to 63, each once within a row
- decode_states: bfloat16 [16, 8192], P('group'), may hold values from -6 to 6
- query_weight: bfloat16 [8192, 8192], P(None, 'tensor'), may hold values from -0.0625 to 0.0625
- cache_keys: bfloat16 [16, 4096, 1024], P('group', 'tensor'), may hold values from -606 to 606
- cache_values: bfloat16 [16, 4096, 1024], P('group', 'tensor'), may hold values from -6 to 6
- cached_length: int32 [16], P('group'), may hold values from 1 to 4096
Outputs:
- attention_out: bfloat16 [16, 8192], P('group', 'tensor')
Inputs may be any that keep to these rules, and one draw needn't show every extreme that they name: For every group g and block t, page_slot[g, t, :] is a permutation of 0 to 63.
All inputs are finite; a program needn't handle non-finite values.
Results may differ from a plain program's by a relative error of at most 0.017.
Values may be sent and summed in bfloat16 or wider, within the bound.
A program may use at most 192 MiB of HBM per device.

v0:
```python
import jax
import jax.numpy as jnp
from jax import lax
from jax.sharding import PartitionSpec as P

HEAD_WIDTH = 128
PAGE = 8


rope_theta = 500000.0
masked_score = -1e30


def combined_all(array, axis, combine):
    everything = jax.tree.map(lambda part: lax.all_gather(part, axis), array)
    leading = jax.tree.map(lambda part: part[0], everything)

    def turn(k, so_far):
        return combine(so_far, jax.tree.map(lambda part: part[k], everything))

    return lax.fori_loop(1, lax.axis_size(axis), turn, leading)


def apply_rotary(vectors, positions):
    half_width = vectors.shape[-1] // 2
    index_float = jnp.arange(half_width, dtype=jnp.float32)
    frequency = rope_theta ** (-2.0 * index_float / vectors.shape[-1])
    angles = positions[..., None].astype(jnp.float32) * frequency
    cosine_part = jnp.cos(angles)
    sine_part = jnp.sin(angles)
    first_half = vectors[..., :half_width]
    second_half = vectors[..., half_width:]
    return jnp.concatenate(
        [
            first_half * cosine_part - second_half * sine_part,
            second_half * cosine_part + first_half * sine_part,
        ],
        axis=-1,
    )


def combine(earlier, later):
    joint_peak = jnp.maximum(earlier[0], later[0])
    first_scale = jnp.exp(earlier[0] - joint_peak)
    second_scale = jnp.exp(later[0] - joint_peak)
    return (
        joint_peak,
        earlier[1] * first_scale + later[1] * second_scale,
        earlier[2] * first_scale[..., None] + later[2] * second_scale[..., None],
    )


def per_device(
    prefill_states,
    key_weight,
    value_weight,
    page_slot,
    decode_states,
    query_weight,
    cache_keys,
    cache_values,
    cached_length,
):
    tensor_size = lax.axis_size("tensor")
    tensor_rank = lax.axis_index("tensor")
    rows_total = prefill_states.shape[0]
    fresh_count = rows_total // tensor_size
    kv_width = key_weight.shape[1]
    kv_heads = kv_width // HEAD_WIDTH
    joined = jnp.concatenate([key_weight, value_weight], axis=1)
    projected = lax.psum_scatter(
        jnp.dot(prefill_states, joined, preferred_element_type=jnp.float32),
        "tensor",
        scatter_dimension=0,
        tiled=True,
    )
    fresh_keys = projected[:, :kv_width]
    fresh_values = projected[:, kv_width:]
    fresh_keys = fresh_keys.astype(jnp.bfloat16)
    fresh_values = fresh_values.astype(jnp.bfloat16)
    page_count = fresh_count // PAGE
    slot_order = page_slot.reshape(page_count)
    picker = (slot_order[None, :] == jnp.arange(page_count, dtype=jnp.int32)[:, None]).astype(
        jnp.bfloat16
    )
    sorted_keys = jnp.dot(
        picker, fresh_keys.reshape(page_count, PAGE * kv_width), preferred_element_type=jnp.float32
    ).astype(jnp.bfloat16)
    sorted_values = jnp.dot(
        picker,
        fresh_values.reshape(page_count, PAGE * kv_width),
        preferred_element_type=jnp.float32,
    ).astype(jnp.bfloat16)
    moved_keys, moved_values = (
        lax.all_to_all(sorted_keys, "group", split_axis=0, concat_axis=0, tiled=True),
        lax.all_to_all(sorted_values, "group", split_axis=0, concat_axis=0, tiled=True),
    )
    decode_rows = decode_states.shape[0]
    fresh_per_row = fresh_count // decode_rows
    fresh_position_index = (
        cached_length[:, None]
        + tensor_rank * fresh_per_row
        + jnp.arange(fresh_per_row, dtype=jnp.int32)[None, :]
    )
    placed = moved_keys.reshape(decode_rows, fresh_per_row, kv_heads, HEAD_WIDTH).astype(
        jnp.float32
    )
    incoming_keys = apply_rotary(placed, fresh_position_index[:, :, None]).astype(jnp.bfloat16)
    incoming_values = moved_values.reshape(decode_rows, fresh_per_row, kv_heads, HEAD_WIDTH)
    local_queries = jnp.dot(decode_states, query_weight, preferred_element_type=jnp.float32)
    local_heads = local_queries.shape[1] // HEAD_WIDTH
    query_position = cached_length + tensor_size * fresh_per_row
    local_queries = (
        apply_rotary(
            local_queries.reshape(decode_rows, local_heads, HEAD_WIDTH), query_position[:, None]
        )
        .reshape(decode_rows, local_heads * HEAD_WIDTH)
        .astype(jnp.bfloat16)
    )
    query_vectors = lax.all_gather(local_queries, "tensor", axis=1, tiled=True)
    head_total = query_vectors.shape[1] // HEAD_WIDTH
    group_size = head_total // kv_heads
    grouped = query_vectors.reshape(decode_rows, kv_heads, group_size, HEAD_WIDTH)
    context_dev = cache_keys.shape[1]
    prior_keys = cache_keys.reshape(decode_rows, context_dev, kv_heads, HEAD_WIDTH)
    prior_values = cache_values.reshape(decode_rows, context_dev, kv_heads, HEAD_WIDTH)
    inv_scale = 1.0 / HEAD_WIDTH**0.5
    old_scores = (
        jnp.einsum("bhgd,blhd->bhgl", grouped, prior_keys, preferred_element_type=jnp.float32)
        * inv_scale
    )
    new_scores = (
        jnp.einsum("bhgd,blhd->bhgl", grouped, incoming_keys, preferred_element_type=jnp.float32)
        * inv_scale
    )
    usable = (tensor_rank * context_dev + jnp.arange(context_dev, dtype=jnp.int32))[
        None, :
    ] < cached_length[:, None]
    old_scores = jnp.where(usable[:, None, None, :], old_scores, masked_score)
    row_peak = jnp.maximum(jnp.max(old_scores, axis=-1), jnp.max(new_scores, axis=-1))
    old_weights = jnp.exp(old_scores - row_peak[..., None])
    new_weights = jnp.exp(new_scores - row_peak[..., None])
    row_total = jnp.sum(old_weights, axis=-1) + jnp.sum(new_weights, axis=-1)
    weighted = jnp.einsum(
        "bhgl,blhd->bhgd",
        old_weights.astype(jnp.bfloat16),
        prior_values,
        preferred_element_type=jnp.float32,
    )
    weighted = weighted + jnp.einsum(
        "bhgl,blhd->bhgd",
        new_weights.astype(jnp.bfloat16),
        incoming_values,
        preferred_element_type=jnp.float32,
    )
    row_peak = row_peak.reshape(decode_rows, head_total)
    row_total = row_total.reshape(decode_rows, head_total)
    weighted = weighted.reshape(decode_rows, head_total, HEAD_WIDTH)
    row_peak, row_total, weighted = combined_all((row_peak, row_total, weighted), "tensor", combine)
    blended = weighted / row_total[..., None]
    own_heads = lax.dynamic_slice_in_dim(blended, tensor_rank * local_heads, local_heads, 1)
    return own_heads.reshape(decode_rows, local_heads * HEAD_WIDTH).astype(jnp.bfloat16)


def solution(mesh):
    placed = (
        P("group", "tensor"),
        P("tensor", None),
        P("tensor", None),
        P("group", "tensor", None),
        P("group", None),
        P(None, "tensor"),
        P("group", "tensor", None),
        P("group", "tensor", None),
        P("group"),
    )
    return jax.shard_map(
        per_device, mesh=mesh, in_specs=placed, out_specs=P("group", "tensor"), check_vma=False
    )
```

profile of v0, /device:TPU:0, one launch (start us, length us, event | category | flops | bytes accessed | tf_op | source)
XLA Modules:
  0.0 448.2 jit_solution(16704663515337196621)
XLA Ops:
  6.5 24.5 %convolution_bitcast_fusion = f32[4096,2048]{0,1:T(8,128)} fusion(bf16[4096,1024]{1,0:T(8,128)(2,1)} %param.11, bf16[1024,1024]{1,0:T(8,128)(2,1)} %param.13, bf16[1024,1024]{1,0:T(8,128)(2,1)} %param.12), kind=kOutput, calls=%fused_computation.8 | convolution fusion | flops 17188257792 | bytes 46137344 | tf_op jit(solution)/shard_map/dot_general | solution.py:72
  31.1 8.0 %convolution_bitcast_fusion.1 = f32[1,4,8,128]{3,1,2,0:T(4,128)S(1)} fusion(bf16[4,8192]{1,0:T(4,128)(2,1)S(1)} %copy-done, bf16[8192,1024]{1,0:T(8,128)(2,1)} %param.16), kind=kOutput, calls=%fused_computation.27 | convolution fusion | flops 67108864 | bytes 16859136 | tf_op jit(solution)/shard_map/dot_general | solution.py:110
  39.2 0.1 multiply_cosine_fusion.1
  39.3 0.1 subtract_convert_fusion.1
  39.3 0.1 maximum_bitcast_fusion
  39.4 16.1 %all_gather.12 = bf16[4,8192]{1,0:T(4,128)(2,1)S(1)} all-gather(bf16[4,1024]{1,0:T(4,128)(2,1)S(1)} %bitcast.90), channel_id=1, replica_groups=mesh['group'=4,'tensor'=8] {'tensor'}, dimensions={1}, use_global_device_ids=true | all-gather | bytes 73728 | tf_op jit(solution)/shard_map/all_gather | solution.py:120
  55.6 0.1 add_convert_fusion.2
  55.7 1.0 multiply_cosine_fusion
  56.6 303.3 %reduce-scatter.2.cloned.1.call-done = f32[512,2048]{0,1:T(8,128)} async-done(((f32[4096,2048]{0,1:T(8,128)}), f32[512,2048]{0,1:T(8,128)}) %reduce-scatter.2.cloned.1.call-update) | async-done | bytes 4194320 | tf_op jit(solution)/shard_map/reduce_scatter | solution.py:71
  359.9 2.5 convert.19
  362.4 1.1 fusion.48
  363.5 0.5 copy.20
  364.0 0.5 reshape.208
  364.6 1.4 convolution_convert_fusion.1
  366.0 3.7 all-to-all-start
  369.7 0.1 broadcast_compare_fusion
  369.8 3.5 fusion.50
  373.2 1.3 copy.24
  374.5 1.6 reshape.210
  376.1 1.4 convolution_convert_fusion
  377.5 4.0 all-to-all-done
  381.5 4.2 all-to-all-start.1
  385.8 1.5 reshape.212
  387.3 0.7 fusion.49
  388.0 0.8 subtract_convert_fusion
  388.9 0.9 fusion.51
  389.8 9.2 %all-to-all-done.1 = bf16[4,16,8192]{2,1,0:T(8,128)(2,1)} async-done(((bf16[4,16,8192]{2,1,0:T(8,128)(2,1)}), bf16[4,16,8192]{2,1,0:T(8,128)(2,1)}, u32[]{:S(2)}, u32[]{:S(2)}) %all-to-all-start.1) | async-done | bytes 1048608 | tf_op jit(solution)/shard_map/all_to_all | solution.py:96
  399.0 1.6 reshape.211
  400.6 0.4 fusion.27
  401.0 3.6 fusion.21
  404.6 0.1 max.28
  404.7 0.2 fusion.34
  404.9 0.2 fusion.30
  405.2 0.1 add.130
  405.2 13.8 %all_gather.14 = f32[8,4,64]{2,1,0:T(4,128)S(1)} all-gather(f32[1,4,64]{2,1,0:T(4,128)S(1)} %add.130), channel_id=1, replica_groups=mesh['group'=4,'tensor'=8] {'tensor'}, dimensions={0}, use_global_device_ids=true | all-gather | bytes 9216 | tf_op jit(solution)/shard_map/all_gather | solution.py:15
  419.1 12.8 %all_gather.13 = f32[8,4,64]{2,1,0:T(4,128)S(1)} all-gather(f32[1,4,64]{2,1,0:T(4,128)S(1)} %max.28), channel_id=1, replica_groups=mesh['group'=4,'tensor'=8] {'tensor'}, dimensions={0}, use_global_device_ids=true | all-gather | bytes 9216 | tf_op jit(solution)/shard_map/all_gather | solution.py:15
  431.9 0.9 slice_bitcast_fusion
  432.8 7.8 %while.19 = (s32[]{:T(128)}, f32[4,64]{1,0:T(4,128)S(1)}, f32[4,64]{1,0:T(4,128)S(1)}, f32[4,64,128]{2,1,0:T(8,128)S(1)}, f32[8,4,64]{2,1,0:T(4,128)S(1)}, /*ind...) while((s32[]{:T(128)}, f32[4,64]{1,0:T(4,128)S(1)}, ...), condition=%wide.region_6.7_spmd, body=%wide.region_5.6_spmd.sunk | while | flops 99845 | bytes 403607 | solution.py:21
  432.8 1.1 fusion.62
  433.9 1.1 fusion.62
  435.1 1.1 fusion.62
  436.2 1.1 fusion.62
  437.3 1.1 fusion.62
  438.4 1.1 fusion.62
  439.5 1.1 fusion.62
  440.6 0.1 constant_dynamic-slice_fusion
  440.7 0.1 fusion.44
  440.8 0.6 copy.74
  (31 shorter events, 0.3 us)
Async XLA Ops:
  6.5 24.5 %copy-start = (bf16[4,8192]{1,0:T(4,128)(2,1)S(1)}, bf16[4,8192]{1,0:T(4,128)(2,1)}, u32[]{:S(2)}) copy-start(bf16[4,8192]{1,0:T(4,128)(2,1)} %param.15) | copy-start | bytes 196612
  6.5 353.4 %reduce-scatter.2.cloned.1.call-start = ((), (), s32[]{:S(2)}) async-start(), calls=%async_computation.3 | async-start | bytes 37748736 | tf_op jit(solution)/shard_map/reduce_scatter | solution.py:71
  31.1 8.1 %copy-start.4 = (s32[4]{0:T(128)S(1)}, s32[4]{0:T(128)}, u32[]{:S(2)}) copy-start(s32[4]{0:T(128)} %param.19) | copy-start | bytes 52
  362.4 2.2 copy-start.3
  364.6 8.6 %copy-start.2 = (bf16[512,1024]{0,1:T(8,128)(2,1)S(1)}, bf16[512,1024]{0,1:T(8,128)(2,1)}, u32[]{:S(2)}) copy-start(bf16[512,1024]{0,1:T(8,128)(2,1)} %get-tuple-element.204) | copy-start | bytes 3145732
  366.0 15.5 %all-to-all-start = ((bf16[4,16,8192]{2,1,0:T(8,128)(2,1)}), bf16[4,16,8192]{2,1,0:T(8,128)(2,1)S(1)}, u32[]{:S(2)}, u32[]{:S(2)}) async-start(bf16[4,16,8192]{2,1,0:T(8,128)(2,1)} %bitcast.5), calls=%async_computation.1 | async-start | bytes 2097152 | tf_op jit(solution)/shard_map/all_to_all | solution.py:95
  381.5 4.3 copy-start.1
  381.5 17.5 %all-to-all-start.1 = ((bf16[4,16,8192]{2,1,0:T(8,128)(2,1)}), bf16[4,16,8192]{2,1,0:T(8,128)(2,1)}, u32[]{:S(2)}, u32[]{:S(2)}) async-start(bf16[4,16,8192]{2,1,0:T(8,128)(2,1)} %bitcast.8), calls=%async_computation.2 | async-start | bytes 2097152 | tf_op jit(solution)/shard_map/all_to_all | solution.py:96
  385.8 46.1 %all-gather.2.cloned.1.call-start = ((), (), s32[]{:S(2)}) async-start(), calls=%async_computation.4 | async-start | bytes 1179648 | tf_op jit(solution)/shard_map/all_gather | solution.py:15
Sparse Core Ops, SparseCore 0:
  31.2 328.6 reduce-scatter.1
  404.7 22.3 all-gather.1
where the time goes:
time: 449 us; the launch traced here: 448 us
  waiting for transfers between devices  316 us (70%)
  matrix products  43.7 us (10%)
  blocking collectives  42.7 us (10%)
  between operations  13.6 us (3%)
  other arithmetic  12.9 us (3%)
  local copies, waits for them, and re-layouts  10.6 us (2%)
  starting transfers between devices  7.99 us (2%)
    reduce_scatter x1, waiting for transfers between devices, per_device(): lax.psum_scatter(jnp.dot(prefill_states, joined, preferred_element_type=j...  303 us
    all_gather x2, blocking collectives, combined_all(): everything = jax.tree.map(lambda part: lax.all_gather(part, axis), array)  26.6 us
    dot_general x1, matrix products, per_device(): jnp.dot(prefill_states, joined, preferred_element_type=jnp.float32)  24.5 us
    all_gather x1, blocking collectives, per_device(): query_vectors = lax.all_gather(local_queries, 'tensor', axis=1, tiled=True)  16.1 us
    all_to_all x1, waiting for transfers between devices, per_device(): lax.all_to_all(sorted_values, 'group', split_axis=0, concat_axis=0, tiled...  9.2 us
  transfers between devices with their start and end apart: 4, of which 3 were waited for; matrix products, arithmetic and copies ran while one was open for 5% of the time, Pallas kernels for 0%

commit v1 on v0

v1 whole, which is shorter than its diff:
```python
import functools

import jax
import jax.numpy as jnp
from jax import lax
from jax.experimental import pallas as pl
from jax.experimental.pallas import tpu as pltpu
from jax.sharding import PartitionSpec as P

HEAD_WIDTH = 128
PAGE = 8


rope_theta = 500000.0
masked_score = -1e30


def angles_of(positions):
    half_width = HEAD_WIDTH // 2
    index_float = jnp.arange(half_width, dtype=jnp.float32)
    frequency = rope_theta ** (-2.0 * index_float / HEAD_WIDTH)
    return positions[..., None].astype(jnp.float32) * frequency


def full_tables(positions):
    angles = angles_of(positions)
    cosine_part = jnp.cos(angles)
    sine_part = jnp.sin(angles)
    return (
        jnp.concatenate([cosine_part, cosine_part], axis=-1),
        jnp.concatenate([sine_part, sine_part], axis=-1),
    )


def apply_rotary(vectors, positions):
    half_width = vectors.shape[-1] // 2
    angles = angles_of(positions)
    cosine_part = jnp.cos(angles)
    sine_part = jnp.sin(angles)
    first_half = vectors[..., :half_width]
    second_half = vectors[..., half_width:]
    return jnp.concatenate(
        [
            first_half * cosine_part - second_half * sine_part,
            second_half * cosine_part + first_half * sine_part,
        ],
        axis=-1,
    )


def score_kernel(
    blocks, owners, order, x_ref, weight, queries, base_cos, base_sin, step_cos, step_sin,
    scores, sorted_x, held, sems,
):
    block = pl.program_id(0)
    fresh_count = held.shape[1]
    pages = fresh_count // PAGE
    share = fresh_count // owners
    kv_heads = weight.shape[1] // HEAD_WIDTH

    def fetch(which, slot):
        def one(s, carry):
            page = order[which * pages + s]
            start = pl.multiple_of(which * fresh_count + page * PAGE, PAGE)
            pltpu.make_async_copy(
                x_ref.at[pl.ds(start, PAGE), :],
                held.at[slot, pl.ds(pl.multiple_of(s * PAGE, PAGE), PAGE), :],
                sems.at[slot],
            ).start()
            return carry

        lax.fori_loop(0, pages, one, 0, unroll=8)

    slot = lax.rem(block, 2)

    @pl.when(block == 0)
    def _():
        fetch(0, 0)

    @pl.when(block + 1 < blocks)
    def _():
        fetch(block + 1, 1 - slot)

    pltpu.make_async_copy(x_ref.at[pl.ds(0, fresh_count), :], held.at[slot], sems.at[slot]).wait()
    x = held[slot]
    sorted_x[...] = x
    lane = lax.broadcasted_iota(jnp.int32, (share, HEAD_WIDTH), 1)
    sign = jnp.where(lane < HEAD_WIDTH // 2, -1.0, 1.0).astype(jnp.float32)
    small_cos, small_sin = step_cos[...], step_sin[...]
    for o in range(owners):
        rows = slice(o * share, (o + 1) * share)
        keys = jnp.dot(x[rows], weight[...], preferred_element_type=jnp.float32)
        big_cos = base_cos[0, o : o + 1, :]
        big_sin = base_sin[0, o : o + 1, :]
        cosine = big_cos * small_cos - big_sin * small_sin
        sine = (big_sin * small_cos + big_cos * small_sin) * sign
        turned = []
        for h in range(kv_heads):
            head = keys[:, h * HEAD_WIDTH : (h + 1) * HEAD_WIDTH]
            turned.append(
                (head * cosine + pltpu.roll(head, HEAD_WIDTH // 2, 1) * sine).astype(jnp.bfloat16)
            )
        turned = jnp.concatenate(turned, axis=1)
        scores[0, o] = lax.dot_general(
            queries[o], turned, (((1,), (1,)), ((), ())), preferred_element_type=jnp.float32
        )


def fresh_scores(order, x, weight, queries, base_cos, base_sin, step_cos, step_sin):
    blocks, owners = base_cos.shape[:2]
    tokens, features = x.shape
    fresh_count = tokens // blocks
    share = fresh_count // owners
    heads = queries.shape[1]
    whole = lambda a: pl.BlockSpec(a.shape, lambda t, order: (0,) * a.ndim)
    per_block = lambda a: pl.BlockSpec((1,) + a.shape[1:], lambda t, order: (t, 0, 0))
    return pl.pallas_call(
        functools.partial(score_kernel, blocks, owners),
        grid_spec=pltpu.PrefetchScalarGridSpec(
            num_scalar_prefetch=1,
            grid=(blocks,),
            in_specs=[
                pl.BlockSpec(memory_space=pltpu.HBM),
                whole(weight),
                whole(queries),
                per_block(base_cos),
                per_block(base_sin),
                whole(step_cos),
                whole(step_sin),
            ],
            out_specs=[
                pl.BlockSpec((1, owners, heads, share), lambda t, order: (t, 0, 0, 0)),
                pl.BlockSpec((fresh_count, features), lambda t, order: (t, 0)),
            ],
            scratch_shapes=[
                pltpu.VMEM((2, fresh_count, features), jnp.bfloat16),
                pltpu.SemaphoreType.DMA((2,)),
            ],
        ),
        out_shape=[
            jax.ShapeDtypeStruct((blocks, owners, heads, share), jnp.float32),
            jax.ShapeDtypeStruct((tokens, features), jnp.bfloat16),
        ],
        compiler_params=pltpu.CompilerParams(vmem_limit_bytes=40 * 1024 * 1024),
    )(order, x, weight, queries, base_cos, base_sin, step_cos, step_sin)


def per_device(
    prefill_states,
    key_weight,
    value_weight,
    page_slot,
    decode_states,
    query_weight,
    cache_keys,
    cache_values,
    cached_length,
):
    groups = lax.axis_size("group")
    ranks = lax.axis_size("tensor")
    group = lax.axis_index("group")
    rank = lax.axis_index("tensor")
    tokens, features = prefill_states.shape
    fresh_count = tokens // ranks
    pages = fresh_count // PAGE
    kv_heads = key_weight.shape[1] // HEAD_WIDTH
    rows = decode_states.shape[0]
    share = fresh_count // groups
    span = fresh_count // rows
    senders = span // share
    assert senders * share == span
    own_row = group // senders
    offset = (group % senders) * share
    inv_scale = 1.0 / HEAD_WIDTH**0.5

    local_queries = jnp.dot(decode_states, query_weight, preferred_element_type=jnp.float32)
    local_heads = local_queries.shape[1] // HEAD_WIDTH
    heads = local_heads * ranks
    per_kv = heads // kv_heads
    local_queries = apply_rotary(
        local_queries.reshape(rows, local_heads, HEAD_WIDTH),
        (cached_length + ranks * span)[:, None],
    ).astype(jnp.bfloat16)
    every_query = lax.all_gather(
        local_queries.reshape(rows, local_heads * HEAD_WIDTH), ("group", "tensor")
    )
    every_query = every_query.reshape(groups, ranks, rows, local_heads, HEAD_WIDTH)
    every_length = lax.all_gather(cached_length, "group")
    slots = lax.all_gather(page_slot.reshape(pages), "tensor")

    index = jnp.arange(pages, dtype=jnp.int32)
    order = jnp.sum(
        jnp.where(slots[:, None, :] == index[None, :, None], index[None, None, :], 0), axis=-1
    )
    fresh_length = lax.dynamic_index_in_dim(every_length, own_row, 1, keepdims=False)
    fresh_query = lax.dynamic_index_in_dim(every_query, own_row, 2, keepdims=False)
    fresh_query = fresh_query.reshape(groups, heads, 1, HEAD_WIDTH)
    own_kv = (jnp.arange(heads) // per_kv)[:, None] == jnp.arange(kv_heads)[None, :]
    spread = jnp.where(own_kv[None, :, :, None], fresh_query, jnp.zeros_like(fresh_query))
    spread = spread.reshape(groups, heads, kv_heads * HEAD_WIDTH)
    base = (
        fresh_length[None, :] + jnp.arange(ranks, dtype=jnp.int32)[:, None] * span + offset
    )
    base_cos, base_sin = full_tables(base)
    step_cos, step_sin = full_tables(jnp.arange(share, dtype=jnp.int32))
    partial_scores, sorted_x = fresh_scores(
        order.reshape(-1), prefill_states, key_weight, spread, base_cos, base_sin, step_cos, step_sin
    )
    partial_scores = partial_scores.transpose(2, 0, 1, 3)
    scores = lax.psum_scatter(partial_scores, "tensor", scatter_dimension=0, tiled=True) * inv_scale

    grouped = lax.dynamic_index_in_dim(every_query, group, 0, keepdims=False)
    grouped = grouped.transpose(1, 0, 2, 3).reshape(rows, kv_heads, per_kv, HEAD_WIDTH)
    context_dev = cache_keys.shape[1]
    prior_keys = cache_keys.reshape(rows, context_dev, kv_heads, HEAD_WIDTH)
    prior_values = cache_values.reshape(rows, context_dev, kv_heads, HEAD_WIDTH)
    old_scores = (
        jnp.einsum("bhgd,blhd->bhgl", grouped, prior_keys, preferred_element_type=jnp.float32)
        * inv_scale
    )
    usable = (rank * context_dev + jnp.arange(context_dev, dtype=jnp.int32))[
        None, :
    ] < cached_length[:, None]
    old_scores = jnp.where(usable[:, None, None, :], old_scores, masked_score)
    old_peak = jnp.max(old_scores, axis=-1)
    old_weights = jnp.exp(old_scores - old_peak[..., None])
    old_total = jnp.sum(old_weights, axis=-1)
    old_sum = jnp.einsum(
        "bhgl,blhd->bhgd",
        old_weights.astype(jnp.bfloat16),
        prior_values,
        preferred_element_type=jnp.float32,
    )

    peak = jnp.max(scores, axis=(1, 3))
    weights = jnp.exp(scores - peak[:, None, :, None])
    total = jnp.sum(weights, axis=(1, 3))
    weights = lax.all_gather(weights.astype(jnp.bfloat16), "tensor", axis=0, tiled=True)
    mixed = jnp.einsum(
        "htos,tosf->ohf",
        weights,
        sorted_x.reshape(ranks, groups, share, features),
        preferred_element_type=jnp.float32,
    )
    fresh_sum = jnp.einsum(
        "oknf,fkd->oknd",
        mixed.astype(jnp.bfloat16).reshape(groups, kv_heads, per_kv, features),
        value_weight.reshape(features, kv_heads, HEAD_WIDTH),
        preferred_element_type=jnp.float32,
    ).reshape(groups, heads, HEAD_WIDTH)

    fresh_sum = lax.psum_scatter(fresh_sum, "tensor", scatter_dimension=1, tiled=True)
    fresh_stats = jnp.stack([peak.T, total.T], axis=-1)
    fresh_all = jnp.concatenate([fresh_sum, fresh_stats], axis=-1)
    fresh_all = lax.all_to_all(fresh_all, "group", 0, 0, tiled=True)

    old_all = jnp.concatenate(
        [
            old_sum.reshape(rows, heads, HEAD_WIDTH),
            old_peak.reshape(rows, heads, 1),
            old_total.reshape(rows, heads, 1),
        ],
        axis=-1,
    )
    old_all = lax.all_to_all(
        old_all.reshape(rows, ranks, local_heads, HEAD_WIDTH + 2).transpose(1, 0, 2, 3),
        "tensor", 0, 0, tiled=True,
    )
    fresh_all = fresh_all.reshape(rows, senders, local_heads, HEAD_WIDTH + 2).transpose(1, 0, 2, 3)
    parts = jnp.concatenate([old_all, fresh_all], axis=0)
    peaks = parts[..., HEAD_WIDTH]
    factor = jnp.exp(peaks - jnp.max(peaks, axis=0))
    numerator = jnp.sum(parts[..., :HEAD_WIDTH] * factor[..., None], axis=0)
    denominator = jnp.sum(parts[..., HEAD_WIDTH + 1] * factor, axis=0)
    result = numerator / denominator[..., None]
    return result.reshape(rows, local_heads * HEAD_WIDTH).astype(jnp.bfloat16)


def solution(mesh):
    placed = (
        P("group", "tensor"),
        P("tensor", None),
        P("tensor", None),
        P("group", "tensor", None),
        P("group", None),
        P(None, "tensor"),
        P("group", "tensor", None),
        P("group", "tensor", None),
        P("group"),
    )
    return jax.shard_map(
        per_device, mesh=mesh, in_specs=placed, out_specs=P("group", "tensor"), check_vma=False
    )
```

time: 449 us -> 207 us (0.46)
  waiting for transfers between devices: 316 us -> 48.6 us
  blocking collectives: 42.7 us -> 81.7 us
  matrix products: 43.7 us -> 18.1 us
  Pallas kernels: 0 us -> 22.4 us
  other arithmetic: 12.9 us -> 5.9 us
  starting transfers between devices: 7.99 us -> 3.45 us
    reduce_scatter x1 -> x2, waiting for transfers between devices: 303 us -> 48.6 us  [the longest x1 24.3 us: per_device(): lax.psum_scatter(partial_scores, 'tensor', scatter_dimension=0, tiled=True)]
    dot_general x5 -> x2, matrix products: 28.6 us -> 5.57 us  [the longest x1 4.98 us: per_device(): jnp.einsum('htos,tosf->ohf', weights, sorted_x.reshape(ranks, groups, sha...]
    pallas_call x0 -> x1, Pallas kernels: none -> 22.4 us  [fresh_scores(): pl.pallas_call(functools.partial(score_kernel, blocks, owners), grid_spec...]
    all_gather x3, blocking collectives: 42.7 us -> 64.7 us  [the longest x1 42 us: per_device(): lax.all_gather(local_queries.reshape(rows, local_heads * HEAD_WIDTH), ('g...]
    all_to_all x2 -> x1, waiting for transfers between devices: 13.2 us -> 0.01 us  [per_device(): lax.all_to_all(old_all.reshape(rows, ranks, local_heads, HEAD_WIDTH + 2)....]
    unnamed x0 -> x1, blocking collectives: none -> 8.85 us
    all_to_all x0 -> x1, blocking collectives: none -> 8.18 us  [per_device(): fresh_all = lax.all_to_all(fresh_all, 'group', 0, 0, tiled=True)]
    unnamed x13 -> x21, local copies, waits for them, and re-layouts: 0.65 us -> 8.79 us
  transfers between devices with their start and end apart: 4 -> 3, of which waited for: 3 -> 2; matrix products, arithmetic and copies ran while one was open for 5% -> 5% of each run, Pallas kernels for 0% -> 0%
where the time goes in v1:
time: 207 us; the launch traced here: 206 us
  blocking collectives  81.7 us (39%)
  waiting for transfers between devices  48.6 us (23%)
  Pallas kernels  22.4 us (11%)
  matrix products  18.1 us (9%)
  between operations  14.3 us (7%)
  local copies, waits for them, and re-layouts  11.9 us (6%)
  other arithmetic  5.9 us (3%)
  starting transfers between devices  3.45 us (2%)
    all_gather x1, blocking collectives, per_device(): lax.all_gather(local_queries.reshape(rows, local_heads * HEAD_WIDTH), ('g...  42 us
    reduce_scatter x1, waiting for transfers between devices, per_device(): lax.psum_scatter(partial_scores, 'tensor', scatter_dimension=0, tiled=True)  24.3 us
    reduce_scatter x1, waiting for transfers between devices, per_device(): lax.psum_scatter(fresh_sum, 'tensor', scatter_dimension=1, tiled=True)  24.3 us
    pallas_call x1, Pallas kernels, fresh_scores(): pl.pallas_call(functools.partial(score_kernel, blocks, owners), grid_spec...  22.4 us
    all_gather x1, blocking collectives, per_device(): lax.all_gather(weights.astype(jnp.bfloat16), 'tensor', axis=0, tiled=True)  14 us
    unnamed x1, blocking collectives  8.85 us
    unnamed x21, local copies, waits for them, and re-layouts  8.79 us
    all_gather x1, blocking collectives, per_device(): slots = lax.all_gather(page_slot.reshape(pages), 'tensor')  8.74 us
  transfers between devices with their start and end apart: 3, of which 2 were waited for; matrix products, arithmetic and copies ran while one was open for 5% of the time, Pallas kernels for 0%

profile of v1, /device:TPU:0, one launch (start us, length us, event | category | flops | bytes accessed | tf_op | source)
XLA Modules:
  0.0 206.4 jit_solution(8509853110245760195)
XLA Ops:
  6.6 0.7 add_convert_fusion.2
  7.2 1.2 dynamic-slice
  9.1 0.9 dynamic-update-slice
  10.1 8.8 %all-reduce.1 = s32[4,4]{1,0:T(4,128)S(1)} all-reduce(s32[4,4]{1,0:T(4,128)S(1)} %reshape.234), channel_id=3, replica_groups=mesh['group'=4,'tensor'=8] {'group'}, use_global_device_ids=true, to_apply=%add | all-reduce | flops 16 | bytes 128
  18.9 0.2 dynamic-slice_reduce_fusion
  19.2 0.2 multiply_sine_fusion.1
  19.4 0.1 multiply_cosine_fusion.2
  19.5 8.0 %convolution_bitcast_fusion.1 = f32[1,4,8,128]{3,1,2,0:T(4,128)S(1)} fusion(bf16[4,8192]{1,0:T(4,128)(2,1)S(1)} %copy-done, bf16[8192,1024]{1,0:T(8,128)(2,1)} %param.14), kind=kOutput, calls=%fused_computation.14 | convolution fusion | flops 67108864 | bytes 16859136 | tf_op jit(solution)/shard_map/dot_general | solution.py:176
  27.7 0.1 pad_maximum_fusion.6
  27.8 42.0 %all_gather.15 = bf16[32,4,1024]{2,1,0:T(4,128)(2,1)S(1)} all-gather(bf16[1,4,1024]{2,1,0:T(4,128)(2,1)S(1)} %convert_element_type.53), channel_id=1, replica_groups=mesh['group'=4,'tensor'=8] {'group','tensor'}, dimensions={0}, use_global_device_ids=true | all-gather | bytes 270336 | tf_op jit(solution)/shard_map/all_gather | solution.py:184
  69.7 0.1 reshape.242
  69.9 0.2 broadcast_in_dim.87
  70.2 0.1 broadcast_in_dim.82
  70.4 0.3 multiply_sine_fusion
  70.7 8.7 %all-gather = s32[8,1,64]{2,1,0:T(1,128)S(1)} all-gather(s32[1,1,64]{2,1,0:T(1,128)S(1)} %copy-done.4), channel_id=2, replica_groups=mesh['group'=4,'tensor'=8] {'tensor'}, dimensions={0}, use_global_device_ids=true | all-gather | bytes 2304 | tf_op jit(solution)/shard_map/all_gather | solution.py:189
  79.5 0.2 select_reduce_fusion
  79.8 0.1 pad_maximum_fusion.4
  79.9 0.1 pad_maximum_fusion.1
  80.0 22.4 %shard_map.91 = (f32[8,4,64,128]{3,2,1,0:T(8,128)}, bf16[4096,1024]{1,0:T(8,128)(2,1)S(1)}) custom-call(s32[512]{0:T(512)S(1)} %reshape.228.order, bf16[4096,1024]{1,0:T(8,128)(2,1)} %x_ref.1, bf16[1024,1024]{1,0:T(8,128)(2,1)S(1)} %copy-done.2, bf16[4,64,1024]{2,1,0:T(8,128)(2,1)S(1)} %broadcast_select_fusion.queries, ...), custom_call_target="tpu_custom_call" | custom-call | tf_op jit(solution)/shard_map/pallas_call | solution.py:117
  102.5 3.2 %copy-done.1 = bf16[4096,1024]{1,0:T(8,128)(2,1)} copy-done((bf16[4096,1024]{1,0:T(8,128)(2,1)}, bf16[4096,1024]{1,0:T(8,128)(2,1)S(1)}, u32[]{:S(2)}) %copy-start.1) | copy-done | bytes 8388632
  105.7 2.2 %copy.148 = bf16[128,8,8,128]{3,2,1,0:T(8,128)(2,1)S(1)} copy(bf16[128,8,8,128]{3,1,2,0:T(8,128)(2,1)} %bitcast.96) | data formatting | bytes 4194304
  108.1 3.7 %fusion.36 = (f32[4,8,8]{2,1,0:T(8,128)S(1)}, f32[4,8,8,512]{3,2,1,0:T(8,128)S(1)}) fusion(pred[4,512]{1,0:T(4,128)(4,1)S(1)} %broadcast_compare_fusion, bf16[4,512,1024]{2,1,0:T(8,128)(2,1)} %param.15, bf16[4,8,4,8,128]{4,3,2,1,0:T(8,128)(2,1)S(1)} %reshape.242, s32[]{:T(128)S(6)} %select_n.37), kind=kOutput, calls=%fused_computation.79 | convolution fusion | flops 33947392 | bytes 4787204 | tf_op jit(solution)/shard_map/bhgd,blhd->bhgl/dot_general | solution.py:218
  111.8 0.8 fusion
  112.5 24.3 %reduce-scatter.3.cloned.1.call-done = f32[8,8,4,128]{3,0,2,1:T(8,128)} async-done(((f32[64,8,4,128]{3,0,2,1:T(8,128)}), f32[8,8,4,128]{3,0,2,1:T(8,128)}) %reduce-scatter.3.cloned.1.call-update) | async-done | bytes 131088 | tf_op jit(solution)/shard_map/reduce_scatter | solution.py:210
  136.8 1.0 multiply_reduce_fusion
  137.8 1.1 fusion.29
  138.9 14.0 %all_gather.19 = bf16[64,8,4,128]{3,0,2,1:T(8,128)(2,1)S(1)} all-gather(bf16[8,8,4,128]{3,0,2,1:T(8,128)(2,1)S(1)} %get-tuple-element.12), channel_id=1, replica_groups=mesh['group'=4,'tensor'=8] {'tensor'}, dimensions={0}, use_global_device_ids=true | all-gather | bytes 589824 | tf_op jit(solution)/shard_map/all_gather | solution.py:238
  152.9 5.0 %fusion.9 = bf16[4,8,8,1024]{3,2,1,0:T(8,128)(2,1)S(1)} fusion(bf16[64,8,4,128]{3,0,2,1:T(8,128)(2,1)S(1)} %all_gather.19, bf16[8,4,128,1024]{3,2,1,0:T(8,128)(2,1)} %bitcast.95), kind=kOutput, calls=%fused_computation.10 | convolution fusion | flops 537133056 | bytes 9437184 | tf_op jit(solution)/shard_map/htos,tosf->ohf/dot_general | solution.py:239
  157.9 0.6 fusion.16
  158.5 0.7 copy.179
  159.2 0.2 fusion.20
  159.4 0.3 copy.122
  159.7 0.3 copy.121
  160.0 0.1 maximum_bitcast_fusion
  160.1 0.7 copy.123
  160.8 3.4 %all-to-all-start = ((f32[8,4,8,130]{3,2,1,0:T(8,128)}), f32[8,4,8,130]{3,2,1,0:T(8,128)S(1)}, u32[]{:S(2)}, u32[]{:S(2)}) async-start(f32[8,4,8,130]{3,2,1,0:T(8,128)} %copy.123), calls=%async_computation | async-start | bytes 524288 | tf_op jit(solution)/shard_map/all_to_all | solution.py:265
  164.2 0.1 copy.128
  164.3 0.1 copy.127
  164.4 24.3 %reduce-scatter.5.cloned.1.call-done = f32[4,8,128]{2,1,0:T(8,128)} async-done(((f32[4,64,128]{2,1,0:T(8,128)}), f32[4,8,128]{2,1,0:T(8,128)}) %reduce-scatter.5.cloned.1.call-update) | async-done | bytes 16400 | tf_op jit(solution)/shard_map/reduce_scatter | solution.py:252
  188.7 0.8 pad_maximum_fusion.3
  189.5 8.2 %all_to_all.10 = f32[4,8,130]{2,1,0:T(8,128)S(1)} all-to-all(f32[4,8,130]{2,1,0:T(8,128)S(1)} %pad_maximum_fusion.3), channel_id=1, replica_groups=mesh['group'=4,'tensor'=8] {'group'}, dimensions={0} | all-to-all | bytes 33280 | tf_op jit(solution)/shard_map/all_to_all | solution.py:255
  197.6 0.1 fusion.34
  197.8 0.3 copy.141
  198.1 0.3 copy.142
  198.5 0.2 fusion.32
  198.6 0.1 copy.130
  198.7 0.1 fusion.27
  198.9 0.6 copy.181
  (36 shorter events, 0.9 us)
Async XLA Ops:
  6.5 13.0 %copy-start = (bf16[4,8192]{1,0:T(4,128)(2,1)S(1)}, bf16[4,8192]{1,0:T(4,128)(2,1)}, u32[]{:S(2)}) copy-start(bf16[4,8192]{1,0:T(4,128)(2,1)} %param.13) | copy-start | bytes 196612
  6.5 130.3 %reduce-scatter.3.cloned.1.call-start = ((), (), s32[]{:S(2)}) async-start(), calls=%async_computation.4 | async-start | bytes 1179648 | tf_op jit(solution)/shard_map/reduce_scatter | solution.py:210
  19.5 51.2 %copy-start.4 = (s32[1,1,64]{2,1,0:T(1,128)S(1)}, s32[1,1,64]{2,1,0:T(1,128)}, u32[]{:S(2)}) copy-start(s32[1,1,64]{2,1,0:T(1,128)} %param.12) | copy-start | bytes 772
  27.6 52.5 %copy-start.2 = (bf16[1024,1024]{1,0:T(8,128)(2,1)S(1)}, bf16[1024,1024]{1,0:T(8,128)(2,1)}, u32[]{:S(2)}) copy-start(bf16[1024,1024]{1,0:T(8,128)(2,1)} %weight.1) | copy-start | bytes 6291460
  102.5 3.2 %copy-start.1 = (bf16[4096,1024]{1,0:T(8,128)(2,1)}, bf16[4096,1024]{1,0:T(8,128)(2,1)S(1)}, u32[]{:S(2)}) copy-start(bf16[4096,1024]{1,0:T(8,128)(2,1)S(1)} %get-tuple-element.8) | copy-start | bytes 25165828
  105.7 2.3 %copy-start.5 = (s32[4]{0:T(128)S(1)}, s32[4]{0:T(128)}, u32[]{:S(2)}) copy-start(s32[4]{0:T(128)} %param.17) | copy-start | bytes 52
  105.7 83.0 %reduce-scatter.5.cloned.1.call-start = ((), (), s32[]{:S(2)}) async-start(), calls=%async_computation.5 | async-start | bytes 147456 | tf_op jit(solution)/shard_map/reduce_scatter | solution.py:252
  108.0 3.8 %copy-start.3 = (bf16[4,512,1024]{2,1,0:T(8,128)(2,1)S(1)}, bf16[4,512,1024]{2,1,0:T(8,128)(2,1)}, u32[]{:S(2)}) copy-start(bf16[4,512,1024]{2,1,0:T(8,128)(2,1)} %param.16) | copy-start | bytes 12582916
  160.8 28.7 %all-to-all-start = ((f32[8,4,8,130]{3,2,1,0:T(8,128)}), f32[8,4,8,130]{3,2,1,0:T(8,128)S(1)}, u32[]{:S(2)}, u32[]{:S(2)}) async-start(f32[8,4,8,130]{3,2,1,0:T(8,128)} %copy.123), calls=%async_computation | async-start | bytes 524288 | tf_op jit(solution)/shard_map/all_to_all | solution.py:265
Sparse Core Ops, SparseCore 0:
  105.8 30.9 reduce-scatter.2
  159.3 29.2 reduce-scatter.4

commit v2 on v1

--- a/solution.py
+++ b/solution.py
@@ -101,9 +101,12 @@
                 (head * cosine + pltpu.roll(head, HEAD_WIDTH // 2, 1) * sine).astype(jnp.bfloat16)
             )
         turned = jnp.concatenate(turned, axis=1)
-        scores[0, o] = lax.dot_general(
+        found = lax.dot_general(
             queries[o], turned, (((1,), (1,)), ((), ())), preferred_element_type=jnp.float32
         )
+        local_heads = scores.shape[3]
+        for j in range(scores.shape[0]):
+            scores[j, 0, o] = found[j * local_heads : (j + 1) * local_heads]
 
 
 def fresh_scores(order, x, weight, queries, base_cos, base_sin, step_cos, step_sin):
@@ -129,7 +132,9 @@
                 whole(step_sin),
             ],
             out_specs=[
-                pl.BlockSpec((1, owners, heads, share), lambda t, order: (t, 0, 0, 0)),
+                pl.BlockSpec(
+                    (blocks, 1, owners, heads // blocks, share), lambda t, order: (0, t, 0, 0, 0)
+                ),
                 pl.BlockSpec((fresh_count, features), lambda t, order: (t, 0)),
             ],
             scratch_shapes=[
@@ -138,11 +143,391 @@
             ],
         ),
         out_shape=[
-            jax.ShapeDtypeStruct((blocks, owners, heads, share), jnp.float32),
+            jax.ShapeDtypeStruct((blocks, blocks, owners, heads // blocks, share), jnp.float32),
             jax.ShapeDtypeStruct((tokens, features), jnp.bfloat16),
         ],
         compiler_params=pltpu.CompilerParams(vmem_limit_bytes=40 * 1024 * 1024),
     )(order, x, weight, queries, base_cos, base_sin, step_cos, step_sin)
+
+
+def remote(src, dst, send_sem, recv_sem, group, rank):
+    return pltpu.make_async_remote_copy(
+        src_ref=src,
+        dst_ref=dst,
+        send_sem=send_sem,
+        recv_sem=recv_sem,
+        device_id={"group": group, "tensor": rank},
+        device_id_type=pl.DeviceIdType.MESH,
+    )
+
+
+def greet_all(groups, ranks, group, rank):
+    barrier = pltpu.get_barrier_semaphore()
+    count = groups * ranks
+    own = group * ranks + rank
+
+    def greet(step, carry):
+        peer = lax.rem(own + step, count)
+        pl.semaphore_signal(
+            barrier,
+            inc=1,
+            device_id={"group": peer // ranks, "tensor": lax.rem(peer, ranks)},
+            device_id_type=pl.DeviceIdType.MESH,
+        )
+        return carry
+
+    lax.fori_loop(1, count, greet, 0)
+    pl.semaphore_wait(barrier, count - 1)
+
+
+def gather_kernel(
+    groups, ranks, senders, query, meta, own_query, fresh_query, meta_ranks, meta_groups,
+    send_query, send_fresh, send_ranks, send_groups, got_query, got_fresh, got_ranks, got_groups,
+):
+    group, rank = lax.axis_index("group"), lax.axis_index("tensor")
+    greet_all(groups, ranks, group, rank)
+
+    def to_rank(step):
+        peer = lax.rem(rank + step, ranks)
+        return (
+            remote(
+                meta, meta_ranks.at[rank], send_ranks.at[step], got_ranks.at[rank], group, peer
+            ),
+            remote(
+                query, own_query.at[rank], send_query.at[step], got_query.at[rank], group, peer
+            ),
+        )
+
+    def to_group(step):
+        peer = lax.rem(group + step, groups)
+        return remote(
+            meta, meta_groups.at[group], send_groups.at[step], got_groups.at[group], peer, rank
+        )
+
+    def to_fresh(step):
+        peer_group = lax.rem(group + 1 + step // ranks, groups)
+        peer_rank = lax.rem(rank + step, ranks)
+        return remote(
+            query.at[peer_group // senders],
+            fresh_query.at[group, rank],
+            send_fresh.at[step],
+            got_fresh.at[group, rank],
+            peer_group,
+            peer_rank,
+        )
+
+    for step in range(1, ranks):
+        for copy in to_rank(step):
+            copy.start()
+    for step in range(1, groups):
+        to_group(step).start()
+
+    def start(step, carry):
+        to_fresh(step).start()
+        return carry
+
+    lax.fori_loop(0, (groups - 1) * ranks, start, 0)
+    own_query[rank] = query[...]
+    meta_ranks[rank] = meta[...]
+    meta_groups[group] = meta[...]
+    for step in range(1, ranks):
+        source = lax.rem(rank + step, ranks)
+        remote(
+            query, own_query.at[source], send_query.at[step], got_query.at[source], group, source
+        ).wait_recv()
+        remote(
+            meta, meta_ranks.at[source], send_ranks.at[step], got_ranks.at[source], group, source
+        ).wait_recv()
+    for step in range(1, groups):
+        source = lax.rem(group + step, groups)
+        remote(
+            meta, meta_groups.at[source], send_groups.at[step], got_groups.at[source], source, rank
+        ).wait_recv()
+    for t in range(ranks):
+        fresh_query[group, t] = own_query[t, group // senders]
+
+    def finish(step, carry):
+        source_group = lax.rem(group + 1 + step // ranks, groups)
+        source_rank = lax.rem(rank + step, ranks)
+        remote(
+            query.at[0],
+            fresh_query.at[source_group, source_rank],
+            send_fresh.at[step],
+            got_fresh.at[source_group, source_rank],
+            source_group,
+            source_rank,
+        ).wait_recv()
+        to_fresh(step).wait_send()
+        return carry
+
+    lax.fori_loop(0, (groups - 1) * ranks, finish, 0)
+    for step in range(1, ranks):
+        for copy in to_rank(step):
+            copy.wait_send()
+    for step in range(1, groups):
+        to_group(step).wait_send()
+
+
+def gather_queries(groups, ranks, senders, query, meta):
+    rows, local_heads, width = query.shape
+    dma = pltpu.SemaphoreType.DMA
+    others = (groups - 1) * ranks
+    vmem = pl.BlockSpec(memory_space=pltpu.VMEM)
+    return pl.pallas_call(
+        functools.partial(gather_kernel, groups, ranks, senders),
+        in_specs=[vmem] * 2,
+        out_specs=[vmem] * 4,
+        out_shape=[
+            jax.ShapeDtypeStruct((ranks, rows, local_heads, width), query.dtype),
+            jax.ShapeDtypeStruct((groups, ranks, local_heads, width), query.dtype),
+            jax.ShapeDtypeStruct((ranks,) + meta.shape, meta.dtype),
+            jax.ShapeDtypeStruct((groups,) + meta.shape, meta.dtype),
+        ],
+        scratch_shapes=[
+            dma((ranks,)), dma((others,)), dma((ranks,)), dma((groups,)),
+            dma((ranks,)), dma((groups, ranks)), dma((ranks,)), dma((groups,)),
+        ],
+        compiler_params=pltpu.CompilerParams(collective_id=0, has_side_effects=True),
+    )(query, meta)
+
+
+def weight_kernel(
+    ranks, scale, partial_scores, weights, stats, paired, chip_sums, incoming,
+    send_pair, send_sum, send_weight, send_on, got_pair, got_sum, got_weight,
+):
+    group, rank = lax.axis_index("group"), lax.axis_index("tensor")
+    chips = ranks // 2
+    core, chip = lax.rem(rank, 2), rank // 2
+    partner = chip * 2 + 1 - core
+    barrier = pltpu.get_barrier_semaphore()
+
+    def peer_of(step):
+        other = lax.rem(chip + step, chips)
+        return other, other * 2 + core
+
+    for peer in [partner] + [peer_of(step)[1] for step in range(1, chips)]:
+        pl.semaphore_signal(
+            barrier,
+            inc=1,
+            device_id={"group": group, "tensor": peer},
+            device_id_type=pl.DeviceIdType.MESH,
+        )
+    pl.semaphore_wait(barrier, chips)
+
+    order = list(range(1, chips)) + [0]
+
+    def pair_copy(step):
+        other = lax.rem(chip + step, chips)
+        return remote(
+            partial_scores.at[other * 2 + 1 - core],
+            paired.at[other],
+            send_pair.at[other],
+            got_pair.at[other],
+            group,
+            partner,
+        )
+
+    def sum_copy(step):
+        other, peer = peer_of(step)
+        return remote(
+            chip_sums.at[other], incoming.at[chip], send_sum.at[step], got_sum.at[chip], group, peer
+        )
+
+    for step in order:
+        pair_copy(step).start()
+    for step in order:
+        other, peer = peer_of(step)
+        pair_copy(step).wait_recv()
+        chip_sums[other] = partial_scores[peer] + paired[other]
+        if step:
+            sum_copy(step).start()
+    total = chip_sums[chip]
+    for step in range(1, chips):
+        other, peer = peer_of(step)
+        remote(
+            chip_sums.at[other], incoming.at[other], send_sum.at[step], got_sum.at[other], group, peer
+        ).wait_recv()
+        total = total + incoming[other]
+    total = total * scale
+    peak = jnp.max(jnp.max(total, axis=0), axis=-1, keepdims=True)
+    exact = jnp.exp(total - peak[None])
+    weights[rank] = exact.astype(jnp.bfloat16)
+
+    def weight_copy(step):
+        other, peer = peer_of(step)
+        return remote(
+            weights.at[rank], weights.at[rank], send_weight.at[step], got_weight.at[rank], group, peer
+        )
+
+    def on_copy(step):
+        other, peer = peer_of(step)
+        return remote(
+            weights.at[peer], weights.at[peer], send_on.at[step], got_weight.at[peer], group, partner
+        )
+
+    for step in range(1, chips):
+        weight_copy(step).start()
+    on_copy(0).start()
+    amount = jnp.sum(jnp.sum(exact, axis=0), axis=-1, keepdims=True)
+    lane = lax.broadcasted_iota(jnp.int32, stats.shape, 2)
+    stats[...] = jnp.where(lane == 0, peak, jnp.where(lane == 1, amount, 0.0))
+    for step in range(1, chips):
+        other, peer = peer_of(step)
+        remote(
+            weights.at[peer], weights.at[peer], send_weight.at[step], got_weight.at[peer], group, peer
+        ).wait_recv()
+        on_copy(step).start()
+    for step in range(chips):
+        other = lax.rem(chip + step, chips) * 2 + 1 - core
+        remote(
+            weights.at[other], weights.at[other], send_on.at[step], got_weight.at[other], group, partner
+        ).wait_recv()
+    for step in range(chips):
+        pair_copy(step).wait_send()
+        on_copy(step).wait_send()
+        if step:
+            sum_copy(step).wait_send()
+            weight_copy(step).wait_send()
+
+
+def fresh_weights(partial_scores, scale):
+    ranks, blocks, owners, local_heads, share = partial_scores.shape
+    chips = ranks // 2
+    dma = pltpu.SemaphoreType.DMA
+    vmem = pl.BlockSpec(memory_space=pltpu.VMEM)
+    held = pltpu.VMEM((chips, blocks, owners, local_heads, share), jnp.float32)
+    return pl.pallas_call(
+        functools.partial(weight_kernel, ranks, scale),
+        in_specs=[vmem],
+        out_specs=[vmem] * 2,
+        out_shape=[
+            jax.ShapeDtypeStruct(partial_scores.shape, jnp.bfloat16),
+            jax.ShapeDtypeStruct((owners, local_heads, HEAD_WIDTH), jnp.float32),
+        ],
+        scratch_shapes=[held] * 3 + [dma((chips,))] * 6 + [dma((ranks,))],
+        compiler_params=pltpu.CompilerParams(
+            collective_id=1, has_side_effects=True, vmem_limit_bytes=32 * 1024 * 1024
+        ),
+    )(partial_scores)
+
+
+def blend_kernel(
+    groups, ranks, senders, fresh, stats, old, out, fresh_in, stats_in, old_in,
+    send_fresh, send_stats, send_old, got_fresh, got_stats, got_old,
+):
+    group, rank = lax.axis_index("group"), lax.axis_index("tensor")
+    rows = out.shape[0]
+    count = groups * ranks
+    own = group * ranks + rank
+    greet_all(groups, ranks, group, rank)
+
+    def peer_of(step):
+        peer = lax.rem(own + step, count)
+        return peer // ranks, lax.rem(peer, ranks)
+
+    def fresh_copy(step):
+        peer_group, peer_rank = peer_of(step)
+        return remote(
+            fresh.at[peer_group, peer_rank],
+            fresh_in.at[group, rank],
+            send_fresh.at[step],
+            got_fresh.at[group, rank],
+            peer_group,
+            peer_rank,
+        )
+
+    def stats_copy(step):
+        peer = lax.rem(group + step, groups)
+        return remote(
+            stats.at[peer], stats_in.at[group], send_stats.at[step], got_stats.at[group], peer, rank
+        )
+
+    def old_copy(step):
+        peer = lax.rem(rank + step, ranks)
+        return remote(
+            old.at[peer], old_in.at[rank], send_old.at[step], got_old.at[rank], group, peer
+        )
+
+    for step in range(1, ranks):
+        old_copy(step).start()
+    for step in range(1, groups):
+        stats_copy(step).start()
+
+    def start(step, carry):
+        fresh_copy(step).start()
+        return carry
+
+    lax.fori_loop(1, count, start, 0)
+    old_in[rank] = old[rank]
+    stats_in[group] = stats[group]
+    fresh_in[group, rank] = fresh[group, rank]
+    for step in range(1, ranks):
+        source = lax.rem(rank + step, ranks)
+        remote(
+            old.at[source], old_in.at[source], send_old.at[step], got_old.at[source], group, source
+        ).wait_recv()
+    for step in range(1, groups):
+        source = lax.rem(group + step, groups)
+        remote(
+            stats.at[source], stats_in.at[source], send_stats.at[step], got_stats.at[source], source, rank
+        ).wait_recv()
+
+    def finish(step, carry):
+        source_group, source_rank = peer_of(step)
+        remote(
+            fresh.at[source_group, source_rank],
+            fresh_in.at[source_group, source_rank],
+            send_fresh.at[step],
+            got_fresh.at[source_group, source_rank],
+            source_group,
+            source_rank,
+        ).wait_recv()
+        fresh_copy(step).wait_send()
+        return carry
+
+    lax.fori_loop(1, count, finish, 0)
+    for row in range(rows):
+        peaks, totals, sums = [], [], []
+        for t in range(ranks):
+            about = old_in[t, rows]
+            peaks.append(about[:, row : row + 1])
+            totals.append(about[:, rows + row : rows + row + 1])
+            sums.append(old_in[t, row])
+        for sender in range(row * senders, (row + 1) * senders):
+            about = stats_in[sender]
+            peaks.append(about[:, 0:1])
+            totals.append(about[:, 1:2])
+            sums.append(jnp.sum(fresh_in[sender], axis=0))
+        top = functools.reduce(jnp.maximum, peaks)
+        factors = [jnp.exp(peak - top) for peak in peaks]
+        numerator = sum(a * b for a, b in zip(sums, factors))
+        denominator = sum(a * b for a, b in zip(totals, factors))
+        out[row] = (numerator / denominator).astype(out.dtype)
+    for step in range(1, ranks):
+        old_copy(step).wait_send()
+    for step in range(1, groups):
+        stats_copy(step).wait_send()
+
+
+def blend(senders, fresh, stats, old):
+    groups, ranks, local_heads, width = fresh.shape
+    rows = old.shape[1] - 1
+    dma = pltpu.SemaphoreType.DMA
+    vmem = pl.BlockSpec(memory_space=pltpu.VMEM)
+    return pl.pallas_call(
+        functools.partial(blend_kernel, groups, ranks, senders),
+        in_specs=[vmem] * 3,
+        out_specs=vmem,
+        out_shape=jax.ShapeDtypeStruct((rows, local_heads, width), jnp.bfloat16),
+        scratch_shapes=[
+            pltpu.VMEM(fresh.shape, jnp.float32),
+            pltpu.VMEM(stats.shape, jnp.float32),
+            pltpu.VMEM(old.shape, jnp.float32),
+            dma((groups * ranks,)), dma((groups,)), dma((ranks,)),
+            dma((groups, ranks)), dma((groups,)), dma((ranks,)),
+        ],
+        compiler_params=pltpu.CompilerParams(collective_id=2, has_side_effects=True),
+    )(fresh, stats, old)
 
 
 def per_device(
@@ -181,19 +566,26 @@
         local_queries.reshape(rows, local_heads, HEAD_WIDTH),
         (cached_length + ranks * span)[:, None],
     ).astype(jnp.bfloat16)
-    every_query = lax.all_gather(
-        local_queries.reshape(rows, local_heads * HEAD_WIDTH), ("group", "tensor")
-    )
-    every_query = every_query.reshape(groups, ranks, rows, local_heads, HEAD_WIDTH)
-    every_length = lax.all_gather(cached_length, "group")
-    slots = lax.all_gather(page_slot.reshape(pages), "tensor")
+    pad = jnp.zeros((1, HEAD_WIDTH), jnp.int32)
+    meta = jnp.concatenate(
+        [
+            pad.at[0, :pages].set(page_slot.reshape(pages)),
+            pad.at[0, :rows].set(cached_length),
+            jnp.zeros((6, HEAD_WIDTH), jnp.int32),
+        ],
+        axis=0,
+    )
+    own_query, fresh_query, meta_ranks, meta_groups = gather_queries(
+        groups, ranks, senders, local_queries, meta
+    )
+    slots = meta_ranks[:, 0, :pages]
+    every_length = meta_groups[:, 1, :rows]
 
     index = jnp.arange(pages, dtype=jnp.int32)
     order = jnp.sum(
         jnp.where(slots[:, None, :] == index[None, :, None], index[None, None, :], 0), axis=-1
     )
     fresh_length = lax.dynamic_index_in_dim(every_length, own_row, 1, keepdims=False)
-    fresh_query = lax.dynamic_index_in_dim(every_query, own_row, 2, keepdims=False)
     fresh_query = fresh_query.reshape(groups, heads, 1, HEAD_WIDTH)
     own_kv = (jnp.arange(heads) // per_kv)[:, None] == jnp.arange(kv_heads)[None, :]
     spread = jnp.where(own_kv[None, :, :, None], fresh_query, jnp.zeros_like(fresh_query))
@@ -206,11 +598,9 @@
     partial_scores, sorted_x = fresh_scores(
         order.reshape(-1), prefill_states, key_weight, spread, base_cos, base_sin, step_cos, step_sin
     )
-    partial_scores = partial_scores.transpose(2, 0, 1, 3)
-    scores = lax.psum_scatter(partial_scores, "tensor", scatter_dimension=0, tiled=True) * inv_scale
-
-    grouped = lax.dynamic_index_in_dim(every_query, group, 0, keepdims=False)
-    grouped = grouped.transpose(1, 0, 2, 3).reshape(rows, kv_heads, per_kv, HEAD_WIDTH)
+    weights, fresh_stats = fresh_weights(partial_scores, inv_scale)
+
+    grouped = own_query.transpose(1, 0, 2, 3).reshape(rows, kv_heads, per_kv, HEAD_WIDTH)
     context_dev = cache_keys.shape[1]
     prior_keys = cache_keys.reshape(rows, context_dev, kv_heads, HEAD_WIDTH)
     prior_values = cache_values.reshape(rows, context_dev, kv_heads, HEAD_WIDTH)
@@ -232,12 +622,8 @@
         preferred_element_type=jnp.float32,
     )
 
-    peak = jnp.max(scores, axis=(1, 3))
-    weights = jnp.exp(scores - peak[:, None, :, None])
-    total = jnp.sum(weights, axis=(1, 3))
-    weights = lax.all_gather(weights.astype(jnp.bfloat16), "tensor", axis=0, tiled=True)
     mixed = jnp.einsum(
-        "htos,tosf->ohf",
+        "jtois,tosf->ojif",
         weights,
         sorted_x.reshape(ranks, groups, share, features),
         preferred_element_type=jnp.float32,
@@ -247,33 +633,21 @@
         mixed.astype(jnp.bfloat16).reshape(groups, kv_heads, per_kv, features),
         value_weight.reshape(features, kv_heads, HEAD_WIDTH),
         preferred_element_type=jnp.float32,
-    ).reshape(groups, heads, HEAD_WIDTH)
-
-    fresh_sum = lax.psum_scatter(fresh_sum, "tensor", scatter_dimension=1, tiled=True)
-    fresh_stats = jnp.stack([peak.T, total.T], axis=-1)
-    fresh_all = jnp.concatenate([fresh_sum, fresh_stats], axis=-1)
-    fresh_all = lax.all_to_all(fresh_all, "group", 0, 0, tiled=True)
-
+    ).reshape(groups, ranks, local_heads, HEAD_WIDTH)
+
+    about = jnp.concatenate(
+        [old_peak.reshape(rows, heads), old_total.reshape(rows, heads)], axis=0
+    )
+    about = jnp.pad(about.T, ((0, 0), (0, HEAD_WIDTH - 2 * rows)))
     old_all = jnp.concatenate(
         [
-            old_sum.reshape(rows, heads, HEAD_WIDTH),
-            old_peak.reshape(rows, heads, 1),
-            old_total.reshape(rows, heads, 1),
-        ],
-        axis=-1,
-    )
-    old_all = lax.all_to_all(
-        old_all.reshape(rows, ranks, local_heads, HEAD_WIDTH + 2).transpose(1, 0, 2, 3),
-        "tensor", 0, 0, tiled=True,
-    )
-    fresh_all = fresh_all.reshape(rows, senders, local_heads, HEAD_WIDTH + 2).transpose(1, 0, 2, 3)
-    parts = jnp.concatenate([old_all, fresh_all], axis=0)
-    peaks = parts[..., HEAD_WIDTH]
-    factor = jnp.exp(peaks - jnp.max(peaks, axis=0))
-    numerator = jnp.sum(parts[..., :HEAD_WIDTH] * factor[..., None], axis=0)
-    denominator = jnp.sum(parts[..., HEAD_WIDTH + 1] * factor, axis=0)
-    result = numerator / denominator[..., None]
-    return result.reshape(rows, local_heads * HEAD_WIDTH).astype(jnp.bfloat16)
+            old_sum.reshape(rows, ranks, local_heads, HEAD_WIDTH).transpose(1, 0, 2, 3),
+            about.reshape(ranks, 1, local_heads, HEAD_WIDTH),
+        ],
+        axis=1,
+    )
+    result = blend(senders, fresh_sum, fresh_stats, old_all)
+    return result.reshape(rows, local_heads * HEAD_WIDTH)
 
 
 def solution(mesh):

time: 207 us -> 108 us (0.52)
  blocking collectives: 81.7 us -> 0 us
  Pallas kernels: 22.4 us -> 76 us
  waiting for transfers between devices: 48.6 us -> 0 us
  between operations: 14.3 us -> 0.22 us
  local copies, waits for them, and re-layouts: 11.9 us -> 6.34 us
  starting transfers between devices: 3.45 us -> 0 us
    all_gather x3 -> x0, blocking collectives: 64.7 us -> none  [the longest x1 42 us: per_device(): lax.all_gather(local_queries.reshape(rows, local_heads * HEAD_WIDTH), ('g...]
    pallas_call x0 -> x3, Pallas kernels: none -> 54 us  [the longest x1 23.2 us: fresh_weights(): pl.pallas_call(functools.partial(weight_kernel, ranks, scale), in_specs=[...]
    reduce_scatter x2 -> x0, waiting for transfers between devices: 48.6 us -> none  [the longest x1 24.3 us: per_device(): lax.psum_scatter(partial_scores, 'tensor', scatter_dimension=0, tiled=True)]
    unnamed x1 -> x0, blocking collectives: 8.85 us -> none
    all_to_all x1 -> x0, blocking collectives: 8.18 us -> none  [per_device(): fresh_all = lax.all_to_all(fresh_all, 'group', 0, 0, tiled=True)]
    unnamed x21 -> x16, local copies, waits for them, and re-layouts: 8.79 us -> 3.04 us
    dot_general x1, matrix products: 4.98 us -> 1.57 us  [per_device(): jnp.einsum('jtois,tosf->ojif', weights, sorted_x.reshape(ranks, groups, s...]
    all_to_all x1 -> x0, starting transfers between devices: 3.41 us -> none  [per_device(): lax.all_to_all(old_all.reshape(rows, ranks, local_heads, HEAD_WIDTH + 2)....]
  transfers between devices with their start and end apart: 3 -> 0, of which waited for: 2 -> 0; matrix products, arithmetic and copies ran while one was open for 5% -> 0% of each run, Pallas kernels for 0% -> 0%
where the time goes in v2:
time: 108 us; the launch traced here: 107 us
  Pallas kernels  76 us (70%)
  matrix products  17.6 us (16%)
  other arithmetic  6.81 us (6%)
  local copies, waits for them, and re-layouts  6.34 us (6%)
    pallas_call x1, Pallas kernels, fresh_weights(): pl.pallas_call(functools.partial(weight_kernel, ranks, scale), in_specs=[...  23.2 us
    pallas_call x1, Pallas kernels, fresh_scores(): pl.pallas_call(functools.partial(score_kernel, blocks, owners), grid_spec...  22 us
    pallas_call x1, Pallas kernels, blend(): pl.pallas_call(functools.partial(blend_kernel, groups, ranks, senders), i...  16.5 us
    pallas_call x1, Pallas kernels, gather_queries(): pl.pallas_call(functools.partial(gather_kernel, groups, ranks, senders),...  14.2 us
    dot_general x1, matrix products, per_device(): jnp.dot(decode_states, query_weight, preferred_element_type=jnp.float32)  8.08 us
    dot_general x1, matrix products, per_device(): jnp.einsum('bhgd,blhd->bhgl', grouped, prior_keys, preferred_element_type...  3.45 us
    dot_general x1, matrix products, per_device(): jnp.einsum('bhgl,blhd->bhgd', old_weights.astype(jnp.bfloat16), prior_val...  3.24 us
    another operation x5, other arithmetic  3.22 us

profile of v2, /device:TPU:0, one launch (start us, length us, event | category | flops | bytes accessed | tf_op | source)
XLA Modules:
  0.0 107.0 jit_solution(14583765148347462241)
XLA Ops:
  0.0 0.0 copy-start
  0.0 0.6 compare_reduce_fusion
  0.7 1.3 %fusion.35 = (s32[1,4]{1,0:T(1,128)S(1)}, f32[4]{0:T(128)S(1)}) fusion(s32[4]{0:T(128)} %param.21, pred[]{:T(512)} %compare_reduce_fusion), kind=kLoop, calls=%fused_computation.64 | loop fusion | flops 12 | bytes 49 | tf_op jit(solution)/shard_map/reshape.75
  2.0 0.1 multiply_cosine_fusion.2
  2.1 0.0 copy-start.5
  2.1 8.1 %convolution_bitcast_fusion = f32[1,4,8,128]{3,1,2,0:T(4,128)S(1)} fusion(bf16[4,8192]{1,0:T(4,128)(2,1)} %param.17, bf16[8192,1024]{1,0:T(8,128)(2,1)} %param.18), kind=kOutput, calls=%fused_computation.18 | convolution fusion | flops 67108864 | bytes 16859136 | tf_op jit(solution)/shard_map/dot_general | solution.py:561
  10.2 0.1 subtract_convert_fusion
  10.3 0.7 pad_maximum_fusion.5.query
  10.9 0.6 compare_reduce_fusion.1
  11.6 0.0 copy-done.5
  11.6 0.6 fusion.34
  12.2 0.1 pad.28.clone
  12.2 0.7 fusion.33.meta
  12.9 14.2 %shard_map.91 = (bf16[8,4,8,128]{3,2,1,0:T(8,128)(2,1)}, bf16[4,8,8,128]{3,2,1,0:T(8,128)(2,1)}, s32[8,8,128]{2,1,0:T(8,128)}, s32[4,8,128]{2,1,0:T(8,128)}) custom-call(bf16[4,8,128]{2,1,0:T(8,128)(2,1)} %pad_maximum_fusion.5.query, s32[8,128]{1,0:T(8,128)} %fusion.33.meta), custom_call_target="tpu_custom_call" | custom-call | tf_op jit(solution)/shard_map/pallas_call | solution.py:276
  27.1 0.7 slice.47
  27.9 0.2 dynamic-slice_reduce_fusion
  28.1 0.1 add_convert_fusion.1
  28.2 0.2 multiply_sine_fusion.1
  28.4 0.1 pad_maximum_fusion.3
  28.5 0.9 broadcast_in_dim.87
  29.4 0.2 broadcast_in_dim.88
  29.6 0.1 iota_compare_fusion.1
  29.7 0.1 broadcast_in_dim.83
  29.9 0.8 slice.46
  30.7 0.2 select_reduce_fusion
  30.9 0.1 reshape.273.order
  31.0 0.3 multiply_sine_fusion
  31.3 0.1 pad_maximum_fusion.1
  31.4 0.0 copy-start.1
  31.4 1.6 %copy-done.1 = bf16[1024,1024]{1,0:T(8,128)(2,1)S(1)} copy-done((bf16[1024,1024]{1,0:T(8,128)(2,1)S(1)}, bf16[1024,1024]{1,0:T(8,128)(2,1)}, u32[]{:S(2)}) %copy-start.1) | copy-done | bytes 2097176
  33.0 22.0 %shard_map.92 = (f32[8,8,4,8,128]{4,3,2,1,0:T(8,128)S(1)}, bf16[4096,1024]{1,0:T(8,128)(2,1)S(1)}) custom-call(s32[512]{0:T(512)S(1)} %reshape.273.order, bf16[4096,1024]{1,0:T(8,128)(2,1)} %x_ref.1, bf16[1024,1024]{1,0:T(8,128)(2,1)S(1)} %copy-done.1, bf16[4,64,1024]{2,1,0:T(8,128)(2,1)S(1)} %broadcast_select_fusion.queries, ...), custom_call_target="tpu_custom_call" | custom-call | tf_op jit(solution)/shard_map/pallas_call | solution.py:120
  55.1 23.2 %shard_map.93 = (bf16[8,8,4,8,128]{4,3,2,1,0:T(8,128)(2,1)S(1)}, f32[4,8,128]{2,1,0:T(8,128)S(1)}) custom-call(f32[8,8,4,8,128]{4,3,2,1,0:T(8,128)S(1)} %get-tuple-element.40.partial_scores), custom_call_target="tpu_custom_call" | custom-call | tf_op jit(solution)/shard_map/pallas_call | solution.py:399
  78.3 0.0 copy-start.2
  78.3 0.0 copy-start.4
  78.4 1.6 %fusion.14 = bf16[4,8,8,1024]{3,2,0,1:T(8,128)(2,1)S(1)} fusion(bf16[8,4,128,1024]{3,2,1,0:T(8,128)(2,1)S(1)} %bitcast.84, bf16[8,8,4,8,128]{4,3,2,1,0:T(8,128)(2,1)S(1)} %get-tuple-element.41), kind=kOutput, calls=%fused_computation.13 | convolution fusion | flops 537133056 | bytes 9437184 | tf_op jit(solution)/shard_map/jtois,tosf->ojif/dot_general | solution.py:625
  79.9 1.2 %fusion.23.fresh = f32[4,8,8,128]{3,2,1,0:T(8,128)} fusion(bf16[4,8,8,1024]{3,2,0,1:T(8,128)(2,1)S(1)} %fusion.14, bf16[1024,1024]{1,0:T(8,128)(2,1)S(1)} %copy-done), kind=kOutput, calls=%fused_computation.16 | convolution fusion | flops 67108864 | bytes 2752512 | tf_op jit(solution)/shard_map/oknf,fkd->oknd/dot_general | solution.py:631
  81.2 0.0 copy-done.4
  81.2 0.1 broadcast_compare_fusion
  81.3 0.0 copy-done.3
  81.3 3.5 %fusion.36 = (f32[4,8,8]{2,1,0:T(8,128)S(1)}, f32[4,8,8,512]{3,2,1,0:T(8,128)S(1)}) fusion(pred[4,512]{1,0:T(4,128)(4,1)S(1)} %broadcast_compare_fusion, bf16[4,512,1024]{2,1,0:T(8,128)(2,1)} %param.19, bf16[8,4,8,128]{3,2,1,0:T(8,128)(2,1)S(1)} %copy-done.3), kind=kOutput, calls=%fused_computation.69 | convolution fusion | flops 33947392 | bytes 4787200 | tf_op jit(solution)/shard_map/bhgd,blhd->bhgl/dot_general | solution.py:608
  84.7 0.2 fusion.30
  85.0 0.1 reshape.279
  85.1 0.1 reshape.278
  85.2 0.1 copy.43
  85.3 3.2 %fusion.24 = f32[8,4,8,128]{3,2,1,0:T(8,128)S(1)} fusion(bf16[4,8,8,512]{3,2,1,0:T(8,128)(2,1)S(1)} %get-tuple-element.45, bf16[4,512,1024]{2,1,0:T(8,128)(2,1)} %param.20), kind=kOutput, calls=%fused_computation.17 | convolution fusion | flops 33554432 | bytes 4587520 | tf_op jit(solution)/shard_map/bhgl,blhd->bhgd/dot_general | solution.py:618
  88.5 0.7 pad_maximum_fusion.old
  89.2 16.5 %shard_map.94 = bf16[4,8,128]{2,1,0:T(8,128)(2,1)} custom-call(f32[4,8,8,128]{3,2,1,0:T(8,128)} %fusion.23.fresh, f32[4,8,128]{2,1,0:T(8,128)} %copy-done.2, f32[8,5,8,128]{3,2,1,0:T(8,128)} %pad_maximum_fusion.old), custom_call_target="tpu_custom_call" | custom-call | tf_op jit(solution)/shard_map/pallas_call | solution.py:517
  105.7 1.3 %copy.95 = bf16[1,4,8,128]{3,1,2,0:T(4,128)(2,1)} copy(bf16[1,4,8,128]{3,2,1,0:T(8,128)(2,1)} %bitcast.89) | data formatting | bytes 16384
  (14 shorter events, 0.1 us)
Async XLA Ops:
  0.0 79.9 %copy-start = (bf16[1024,1024]{1,0:T(8,128)(2,1)S(1)}, bf16[1024,1024]{1,0:T(8,128)(2,1)}, u32[]{:S(2)}) copy-start(bf16[1024,1024]{1,0:T(8,128)(2,1)} %param.15) | copy-start | bytes 6291460
  2.1 9.5 %copy-start.5 = (s32[1,1,64]{2,1,0:T(1,128)S(1)}, s32[1,1,64]{2,1,0:T(1,128)}, u32[]{:S(2)}) copy-start(s32[1,1,64]{2,1,0:T(1,128)} %param.16) | copy-start | bytes 772
  31.4 1.6 %copy-start.1 = (bf16[1024,1024]{1,0:T(8,128)(2,1)S(1)}, bf16[1024,1024]{1,0:T(8,128)(2,1)}, u32[]{:S(2)}) copy-start(bf16[1024,1024]{1,0:T(8,128)(2,1)} %weight.1) | copy-start | bytes 6291460
  78.3 1.6 %copy-start.2 = (f32[4,8,128]{2,1,0:T(8,128)}, f32[4,8,128]{2,1,0:T(8,128)S(1)}, u32[]{:S(2)}) copy-start(f32[4,8,128]{2,1,0:T(8,128)S(1)} %get-tuple-element.43.stats) | copy-start | bytes 49156
  78.3 2.9 %copy-start.4 = (s32[4]{0:T(128)S(1)}, s32[4]{0:T(128)}, u32[]{:S(2)}) copy-start(s32[4]{0:T(128)} %param.21) | copy-start | bytes 52
  78.3 2.9 %copy-start.3 = (bf16[8,4,8,128]{3,2,1,0:T(8,128)(2,1)S(1)}, bf16[8,4,8,128]{3,2,1,0:T(8,128)(2,1)}, u32[]{:S(2)}) copy-start(bf16[8,4,8,128]{3,2,1,0:T(8,128)(2,1)} %get-tuple-element.44) | copy-start | bytes 196612

commit v3 on v2

--- a/solution.py
+++ b/solution.py
@@ -48,108 +48,6 @@
     )
 
 
-def score_kernel(
-    blocks, owners, order, x_ref, weight, queries, base_cos, base_sin, step_cos, step_sin,
-    scores, sorted_x, held, sems,
-):
-    block = pl.program_id(0)
-    fresh_count = held.shape[1]
-    pages = fresh_count // PAGE
-    share = fresh_count // owners
-    kv_heads = weight.shape[1] // HEAD_WIDTH
-
-    def fetch(which, slot):
-        def one(s, carry):
-            page = order[which * pages + s]
-            start = pl.multiple_of(which * fresh_count + page * PAGE, PAGE)
-            pltpu.make_async_copy(
-                x_ref.at[pl.ds(start, PAGE), :],
-                held.at[slot, pl.ds(pl.multiple_of(s * PAGE, PAGE), PAGE), :],
-                sems.at[slot],
-            ).start()
-            return carry
-
-        lax.fori_loop(0, pages, one, 0, unroll=8)
-
-    slot = lax.rem(block, 2)
-
-    @pl.when(block == 0)
-    def _():
-        fetch(0, 0)
-
-    @pl.when(block + 1 < blocks)
-    def _():
-        fetch(block + 1, 1 - slot)
-
-    pltpu.make_async_copy(x_ref.at[pl.ds(0, fresh_count), :], held.at[slot], sems.at[slot]).wait()
-    x = held[slot]
-    sorted_x[...] = x
-    lane = lax.broadcasted_iota(jnp.int32, (share, HEAD_WIDTH), 1)
-    sign = jnp.where(lane < HEAD_WIDTH // 2, -1.0, 1.0).astype(jnp.float32)
-    small_cos, small_sin = step_cos[...], step_sin[...]
-    for o in range(owners):
-        rows = slice(o * share, (o + 1) * share)
-        keys = jnp.dot(x[rows], weight[...], preferred_element_type=jnp.float32)
-        big_cos = base_cos[0, o : o + 1, :]
-        big_sin = base_sin[0, o : o + 1, :]
-        cosine = big_cos * small_cos - big_sin * small_sin
-        sine = (big_sin * small_cos + big_cos * small_sin) * sign
-        turned = []
-        for h in range(kv_heads):
-            head = keys[:, h * HEAD_WIDTH : (h + 1) * HEAD_WIDTH]
-            turned.append(
-                (head * cosine + pltpu.roll(head, HEAD_WIDTH // 2, 1) * sine).astype(jnp.bfloat16)
-            )
-        turned = jnp.concatenate(turned, axis=1)
-        found = lax.dot_general(
-            queries[o], turned, (((1,), (1,)), ((), ())), preferred_element_type=jnp.float32
-        )
-        local_heads = scores.shape[3]
-        for j in range(scores.shape[0]):
-            scores[j, 0, o] = found[j * local_heads : (j + 1) * local_heads]
-
-
-def fresh_scores(order, x, weight, queries, base_cos, base_sin, step_cos, step_sin):
-    blocks, owners = base_cos.shape[:2]
-    tokens, features = x.shape
-    fresh_count = tokens // blocks
-    share = fresh_count // owners
-    heads = queries.shape[1]
-    whole = lambda a: pl.BlockSpec(a.shape, lambda t, order: (0,) * a.ndim)
-    per_block = lambda a: pl.BlockSpec((1,) + a.shape[1:], lambda t, order: (t, 0, 0))
-    return pl.pallas_call(
-        functools.partial(score_kernel, blocks, owners),
-        grid_spec=pltpu.PrefetchScalarGridSpec(
-            num_scalar_prefetch=1,
-            grid=(blocks,),
-            in_specs=[
-                pl.BlockSpec(memory_space=pltpu.HBM),
-                whole(weight),
-                whole(queries),
-                per_block(base_cos),
-                per_block(base_sin),
-                whole(step_cos),
-                whole(step_sin),
-            ],
-            out_specs=[
-                pl.BlockSpec(
-                    (blocks, 1, owners, heads // blocks, share), lambda t, order: (0, t, 0, 0, 0)
-                ),
-                pl.BlockSpec((fresh_count, features), lambda t, order: (t, 0)),
-            ],
-            scratch_shapes=[
-                pltpu.VMEM((2, fresh_count, features), jnp.bfloat16),
-                pltpu.SemaphoreType.DMA((2,)),
-            ],
-        ),
-        out_shape=[
-            jax.ShapeDtypeStruct((blocks, blocks, owners, heads // blocks, share), jnp.float32),
-            jax.ShapeDtypeStruct((tokens, features), jnp.bfloat16),
-        ],
-        compiler_params=pltpu.CompilerParams(vmem_limit_bytes=40 * 1024 * 1024),
-    )(order, x, weight, queries, base_cos, base_sin, step_cos, step_sin)
-
-
 def remote(src, dst, send_sem, recv_sem, group, rank):
     return pltpu.make_async_remote_copy(
         src_ref=src,
@@ -181,10 +79,28 @@
 
 
 def gather_kernel(
-    groups, ranks, senders, query, meta, own_query, fresh_query, meta_ranks, meta_groups,
+    groups, ranks, senders, query, meta, states, weight,
+    own_query, fresh_query, meta_ranks, meta_groups, keys,
     send_query, send_fresh, send_ranks, send_groups, got_query, got_fresh, got_ranks, got_groups,
+    state_tiles, key_tiles, state_sems, key_sems,
 ):
     group, rank = lax.axis_index("group"), lax.axis_index("tensor")
+    tile = state_tiles.shape[1]
+    tiles = states.shape[0] // tile
+
+    def state_copy(step, slot):
+        start = pl.multiple_of(step * tile, tile)
+        return pltpu.make_async_copy(
+            states.at[pl.ds(start, tile), :], state_tiles.at[slot], state_sems.at[slot]
+        )
+
+    def key_copy(step, slot):
+        start = pl.multiple_of(step * tile, tile)
+        return pltpu.make_async_copy(
+            key_tiles.at[slot], keys.at[pl.ds(start, tile), :], key_sems.at[slot]
+        )
+
+    state_copy(0, 0).start()
     greet_all(groups, ranks, group, rank)
 
     def to_rank(step):
@@ -230,6 +146,29 @@
     own_query[rank] = query[...]
     meta_ranks[rank] = meta[...]
     meta_groups[group] = meta[...]
+
+    def project(step, carry):
+        slot = lax.rem(step, 2)
+
+        @pl.when(step + 1 < tiles)
+        def _():
+            state_copy(step + 1, 1 - slot).start()
+
+        state_copy(step, slot).wait()
+
+        @pl.when(step >= 2)
+        def _():
+            key_copy(step - 2, slot).wait()
+
+        key_tiles[slot] = jnp.dot(
+            state_tiles[slot], weight[...], preferred_element_type=jnp.float32
+        ).astype(jnp.bfloat16)
+        key_copy(step, slot).start()
+        return carry
+
+    lax.fori_loop(0, tiles, project, 0)
+    key_copy(tiles - 2, (tiles - 2) % 2).wait()
+    key_copy(tiles - 1, (tiles - 1) % 2).wait()
     for step in range(1, ranks):
         source = lax.rem(rank + step, ranks)
         remote(
@@ -268,37 +207,64 @@
         to_group(step).wait_send()
 
 
-def gather_queries(groups, ranks, senders, query, meta):
+def gather_queries(groups, ranks, senders, query, meta, states, weight):
     rows, local_heads, width = query.shape
     dma = pltpu.SemaphoreType.DMA
     others = (groups - 1) * ranks
+    tokens, features = states.shape
+    tile = tokens // ranks
+    hbm = pl.BlockSpec(memory_space=pltpu.HBM)
     vmem = pl.BlockSpec(memory_space=pltpu.VMEM)
     return pl.pallas_call(
         functools.partial(gather_kernel, groups, ranks, senders),
-        in_specs=[vmem] * 2,
-        out_specs=[vmem] * 4,
+        in_specs=[vmem, vmem, hbm, vmem],
+        out_specs=[vmem] * 4 + [hbm],
         out_shape=[
             jax.ShapeDtypeStruct((ranks, rows, local_heads, width), query.dtype),
             jax.ShapeDtypeStruct((groups, ranks, local_heads, width), query.dtype),
             jax.ShapeDtypeStruct((ranks,) + meta.shape, meta.dtype),
             jax.ShapeDtypeStruct((groups,) + meta.shape, meta.dtype),
+            jax.ShapeDtypeStruct((tokens, weight.shape[1]), jnp.bfloat16),
         ],
         scratch_shapes=[
             dma((ranks,)), dma((others,)), dma((ranks,)), dma((groups,)),
             dma((ranks,)), dma((groups, ranks)), dma((ranks,)), dma((groups,)),
+            pltpu.VMEM((2, tile, features), jnp.bfloat16),
+            pltpu.VMEM((2, tile, weight.shape[1]), jnp.bfloat16),
+            dma((2,)), dma((2,)),
         ],
-        compiler_params=pltpu.CompilerParams(collective_id=0, has_side_effects=True),
-    )(query, meta)
+        compiler_params=pltpu.CompilerParams(
+            collective_id=0, has_side_effects=True, vmem_limit_bytes=32 * 1024 * 1024
+        ),
+    )(query, meta, states, weight)
 
 
 def weight_kernel(
-    ranks, scale, partial_scores, weights, stats, paired, chip_sums, incoming,
-    send_pair, send_sum, send_weight, send_on, got_pair, got_sum, got_weight,
+    ranks, owners, scale, keys, queries, base_cos, base_sin, step_cos, step_sin, owner_of,
+    cache_keys, cache_values, own_queries, limits,
+    weights, stats, old,
+    partial_scores, paired, chip_sums, incoming, key_tiles, turned, old_keys, old_values,
+    send_pair, send_sum, send_weight, send_on, got_pair, got_sum, got_weight, key_sems, old_sems,
 ):
     group, rank = lax.axis_index("group"), lax.axis_index("tensor")
     chips = ranks // 2
     core, chip = lax.rem(rank, 2), rank // 2
     partner = chip * 2 + 1 - core
+    tile = turned.shape[0]
+    local_heads = weights.shape[2]
+    heads = local_heads * ranks
+    kv_heads = turned.shape[1] // HEAD_WIDTH
+    per_kv = heads // kv_heads
+    rows, context_dev = cache_keys.shape[:2]
+    pages = tile // PAGE
+
+    def key_copy(step, slot):
+        start = pl.multiple_of(step * tile, tile)
+        return pltpu.make_async_copy(
+            keys.at[pl.ds(start, tile), :], key_tiles.at[slot], key_sems.at[slot]
+        )
+
+    key_copy(0, 0).start()
     barrier = pltpu.get_barrier_semaphore()
 
     def peer_of(step):
@@ -312,45 +278,144 @@
             device_id={"group": group, "tensor": peer},
             device_id_type=pl.DeviceIdType.MESH,
         )
+    key_old = pltpu.make_async_copy(cache_keys, old_keys, old_sems.at[0])
+    value_old = pltpu.make_async_copy(cache_values, old_values, old_sems.at[1])
     pl.semaphore_wait(barrier, chips)
 
-    order = list(range(1, chips)) + [0]
-
-    def pair_copy(step):
-        other = lax.rem(chip + step, chips)
-        return remote(
-            partial_scores.at[other * 2 + 1 - core],
-            paired.at[other],
-            send_pair.at[other],
-            got_pair.at[other],
+    def pair_copy(block):
+        return remote(
+            partial_scores.at[1 - core, block],
+            paired.at[block],
+            send_pair.at[block],
+            got_pair.at[block],
             group,
             partner,
         )
 
-    def sum_copy(step):
+    def sum_copy(step, block):
         other, peer = peer_of(step)
         return remote(
-            chip_sums.at[other], incoming.at[chip], send_sum.at[step], got_sum.at[chip], group, peer
-        )
-
-    for step in order:
-        pair_copy(step).start()
-    for step in order:
+            chip_sums.at[other, block],
+            incoming.at[chip, block],
+            send_sum.at[step, block],
+            got_sum.at[chip, block],
+            group,
+            peer,
+        )
+
+    def add_pair(block):
+        pair_copy(block).wait_recv()
+        for step in range(1, chips):
+            other, peer = peer_of(step)
+            chip_sums[other, block] = partial_scores[core, block, other] + paired[block, other]
+            sum_copy(step, block).start()
+        chip_sums[chip, block] = partial_scores[core, block, chip] + paired[block, chip]
+
+    lane = lax.broadcasted_iota(jnp.int32, (1, HEAD_WIDTH), 1)
+    sign = jnp.where(lane < HEAD_WIDTH // 2, -1.0, 1.0).astype(jnp.float32)
+
+    def score(block, carry):
+        slot = lax.rem(block, 2)
+
+        @pl.when(block + 1 < ranks)
+        def _():
+            key_copy(block + 1, 1 - slot).start()
+
+        key_copy(block, slot).wait()
+        span = pl.ds(pl.multiple_of(block * pages, pages), pages)
+        big_cos = base_cos[span, :].reshape(pages, 1, HEAD_WIDTH)
+        big_sin = base_sin[span, :].reshape(pages, 1, HEAD_WIDTH)
+        small_cos = step_cos[...].reshape(1, PAGE, HEAD_WIDTH)
+        small_sin = step_sin[...].reshape(1, PAGE, HEAD_WIDTH)
+        cosine = (big_cos * small_cos - big_sin * small_sin).reshape(tile, HEAD_WIDTH)
+        sine = (big_sin * small_cos + big_cos * small_sin).reshape(tile, HEAD_WIDTH) * sign
+        for h in range(kv_heads):
+            columns = slice(h * HEAD_WIDTH, (h + 1) * HEAD_WIDTH)
+            head = key_tiles[slot, :, columns].astype(jnp.float32)
+            turned[:, columns] = (
+                head * cosine + pltpu.roll(head, HEAD_WIDTH // 2, 1) * sine
+            ).astype(jnp.bfloat16)
+        found = lax.dot_general(
+            queries[...], turned[...], (((1,), (1,)), ((), ())), preferred_element_type=jnp.float32
+        )
+        owner = owner_of[block]
+        kept = jnp.zeros((heads, tile), jnp.float32)
+        for o in range(owners):
+            kept = jnp.where(owner == o, found[o * heads : (o + 1) * heads], kept)
+        for j in range(ranks):
+            partial_scores[j % 2, block, j // 2] = kept[j * local_heads : (j + 1) * local_heads]
+        pair_copy(block).start()
+
+        @pl.when(block > 0)
+        def _():
+            add_pair(block - 1)
+
+        @pl.when(block == 0)
+        def _():
+            key_old.start()
+            value_old.start()
+
+        return carry
+
+    lax.fori_loop(0, ranks, score, 0)
+    add_pair(ranks - 1)
+
+    key_old.wait()
+    value_old.wait()
+    about = jnp.zeros((heads, HEAD_WIDTH), jnp.float32)
+    position = rank * context_dev + lax.broadcasted_iota(jnp.int32, (1, context_dev), 1)
+    for b in range(rows):
+        old_scores = (
+            lax.dot_general(
+                own_queries[b], old_keys[b], (((1,), (1,)), ((), ())),
+                preferred_element_type=jnp.float32,
+            )
+            * scale
+        )
+        old_scores = jnp.where(position < limits[b : b + 1, 0:1], old_scores, masked_score)
+        old_peak = jnp.max(old_scores, axis=-1, keepdims=True)
+        old_exact = jnp.exp(old_scores - old_peak)
+        old_total = jnp.sum(old_exact, axis=-1, keepdims=True)
+        old_sum = jnp.dot(
+            old_exact.astype(jnp.bfloat16), old_values[b], preferred_element_type=jnp.float32
+        )
+        about = jnp.where(lane == b, old_peak, jnp.where(lane == rows + b, old_total, about))
+        for j in range(ranks):
+            h = j * local_heads // per_kv
+            old[j, b] = old_sum[
+                j * local_heads : (j + 1) * local_heads, h * HEAD_WIDTH : (h + 1) * HEAD_WIDTH
+            ]
+    for j in range(ranks):
+        old[j, rows] = about[j * local_heads : (j + 1) * local_heads]
+
+    for step in range(1, chips):
         other, peer = peer_of(step)
-        pair_copy(step).wait_recv()
-        chip_sums[other] = partial_scores[peer] + paired[other]
-        if step:
-            sum_copy(step).start()
+
+        def arrive(block, carry):
+            remote(
+                chip_sums.at[other, block],
+                incoming.at[other, block],
+                send_sum.at[step, block],
+                got_sum.at[other, block],
+                group,
+                peer,
+            ).wait_recv()
+            return carry
+
+        lax.fori_loop(0, ranks, arrive, 0)
     total = chip_sums[chip]
     for step in range(1, chips):
-        other, peer = peer_of(step)
-        remote(
-            chip_sums.at[other], incoming.at[other], send_sum.at[step], got_sum.at[other], group, peer
-        ).wait_recv()
-        total = total + incoming[other]
+        total = total + incoming[peer_of(step)[0]]
     total = total * scale
-    peak = jnp.max(jnp.max(total, axis=0), axis=-1, keepdims=True)
-    exact = jnp.exp(total - peak[None])
+    owner = owner_of[...]
+    peaks = []
+    token_peak = jnp.zeros_like(total)
+    for o in range(owners):
+        kept = jnp.where(owner == o, total, masked_score)
+        peak = jnp.max(jnp.max(kept, axis=0), axis=-1, keepdims=True)
+        peaks.append(peak)
+        token_peak = jnp.where(owner == o, peak[None], token_peak)
+    exact = jnp.exp(total - token_peak)
     weights[rank] = exact.astype(jnp.bfloat16)
 
     def weight_copy(step):
@@ -368,9 +433,11 @@
     for step in range(1, chips):
         weight_copy(step).start()
     on_copy(0).start()
-    amount = jnp.sum(jnp.sum(exact, axis=0), axis=-1, keepdims=True)
-    lane = lax.broadcasted_iota(jnp.int32, stats.shape, 2)
-    stats[...] = jnp.where(lane == 0, peak, jnp.where(lane == 1, amount, 0.0))
+    for o in range(owners):
+        amount = jnp.sum(
+            jnp.sum(jnp.where(owner == o, exact, 0.0), axis=0), axis=-1, keepdims=True
+        )
+        stats[o] = jnp.where(lane == 0, peaks[o], jnp.where(lane == 1, amount, 0.0))
     for step in range(1, chips):
         other, peer = peer_of(step)
         remote(
@@ -382,33 +449,61 @@
         remote(
             weights.at[other], weights.at[other], send_on.at[step], got_weight.at[other], group, partner
         ).wait_recv()
+
+    def sent(block, carry):
+        pair_copy(block).wait_send()
+        for step in range(1, chips):
+            sum_copy(step, block).wait_send()
+        return carry
+
+    lax.fori_loop(0, ranks, sent, 0)
     for step in range(chips):
-        pair_copy(step).wait_send()
         on_copy(step).wait_send()
         if step:
-            sum_copy(step).wait_send()
             weight_copy(step).wait_send()
 
 
-def fresh_weights(partial_scores, scale):
-    ranks, blocks, owners, local_heads, share = partial_scores.shape
+def fresh_weights(
+    ranks, owners, scale, keys, queries, base_cos, base_sin, step_cos, step_sin, owner_of,
+    cache_keys, cache_values, own_queries, limits,
+):
+    tokens, width = keys.shape
+    tile = tokens // ranks
+    rows, heads = own_queries.shape[:2]
+    local_heads = heads // ranks
     chips = ranks // 2
     dma = pltpu.SemaphoreType.DMA
     vmem = pl.BlockSpec(memory_space=pltpu.VMEM)
-    held = pltpu.VMEM((chips, blocks, owners, local_heads, share), jnp.float32)
+    hbm = pl.BlockSpec(memory_space=pltpu.HBM)
+    held = (chips, local_heads, tile)
     return pl.pallas_call(
-        functools.partial(weight_kernel, ranks, scale),
-        in_specs=[vmem],
-        out_specs=[vmem] * 2,
+        functools.partial(weight_kernel, ranks, owners, scale),
+        in_specs=[hbm] + [vmem] * 6 + [hbm] * 2 + [vmem] * 2,
+        out_specs=[vmem] * 3,
         out_shape=[
-            jax.ShapeDtypeStruct(partial_scores.shape, jnp.bfloat16),
+            jax.ShapeDtypeStruct((ranks, ranks, local_heads, tile), jnp.bfloat16),
             jax.ShapeDtypeStruct((owners, local_heads, HEAD_WIDTH), jnp.float32),
+            jax.ShapeDtypeStruct((ranks, rows + 1, local_heads, HEAD_WIDTH), jnp.float32),
         ],
-        scratch_shapes=[held] * 3 + [dma((chips,))] * 6 + [dma((ranks,))],
+        scratch_shapes=[
+            pltpu.VMEM((2, ranks) + held, jnp.float32),
+            pltpu.VMEM((ranks,) + held, jnp.float32),
+            pltpu.VMEM((chips, ranks, local_heads, tile), jnp.float32),
+            pltpu.VMEM((chips, ranks, local_heads, tile), jnp.float32),
+            pltpu.VMEM((2, tile, width), jnp.bfloat16),
+            pltpu.VMEM((tile, width), jnp.bfloat16),
+            pltpu.VMEM(cache_keys.shape, jnp.bfloat16),
+            pltpu.VMEM(cache_values.shape, jnp.bfloat16),
+            dma((ranks,)), dma((chips, ranks)), dma((chips,)), dma((chips,)),
+            dma((ranks,)), dma((chips, ranks)), dma((ranks,)), dma((2,)), dma((2,)),
+        ],
         compiler_params=pltpu.CompilerParams(
-            collective_id=1, has_side_effects=True, vmem_limit_bytes=32 * 1024 * 1024
+            collective_id=1, has_side_effects=True, vmem_limit_bytes=48 * 1024 * 1024
         ),
-    )(partial_scores)
+    )(
+        keys, queries, base_cos, base_sin, step_cos, step_sin, owner_of,
+        cache_keys, cache_values, own_queries, limits,
+    )
 
 
 def blend_kernel(
@@ -575,57 +670,60 @@
         ],
         axis=0,
     )
-    own_query, fresh_query, meta_ranks, meta_groups = gather_queries(
-        groups, ranks, senders, local_queries, meta
+    own_query, fresh_query, meta_ranks, meta_groups, keys = gather_queries(
+        groups, ranks, senders, local_queries, meta, prefill_states, key_weight
     )
     slots = meta_ranks[:, 0, :pages]
     every_length = meta_groups[:, 1, :rows]
 
-    index = jnp.arange(pages, dtype=jnp.int32)
-    order = jnp.sum(
-        jnp.where(slots[:, None, :] == index[None, :, None], index[None, None, :], 0), axis=-1
-    )
+    per_owner = pages // groups
     fresh_length = lax.dynamic_index_in_dim(every_length, own_row, 1, keepdims=False)
-    fresh_query = fresh_query.reshape(groups, heads, 1, HEAD_WIDTH)
+    page_owner = slots // per_owner
+    length_of_page = jnp.sum(
+        jnp.where(
+            page_owner[..., None] == jnp.arange(groups, dtype=jnp.int32), fresh_length, 0
+        ),
+        axis=-1,
+    )
+    base = (
+        length_of_page
+        + jnp.arange(ranks, dtype=jnp.int32)[:, None] * span
+        + offset
+        + (slots % per_owner) * PAGE
+    )
+    base_cos, base_sin = full_tables(base.reshape(-1))
+    step_cos, step_sin = full_tables(jnp.arange(PAGE, dtype=jnp.int32))
+    owner_of = jnp.repeat(page_owner, PAGE, axis=1).reshape(ranks, 1, fresh_count)
     own_kv = (jnp.arange(heads) // per_kv)[:, None] == jnp.arange(kv_heads)[None, :]
-    spread = jnp.where(own_kv[None, :, :, None], fresh_query, jnp.zeros_like(fresh_query))
-    spread = spread.reshape(groups, heads, kv_heads * HEAD_WIDTH)
-    base = (
-        fresh_length[None, :] + jnp.arange(ranks, dtype=jnp.int32)[:, None] * span + offset
-    )
-    base_cos, base_sin = full_tables(base)
-    step_cos, step_sin = full_tables(jnp.arange(share, dtype=jnp.int32))
-    partial_scores, sorted_x = fresh_scores(
-        order.reshape(-1), prefill_states, key_weight, spread, base_cos, base_sin, step_cos, step_sin
-    )
-    weights, fresh_stats = fresh_weights(partial_scores, inv_scale)
-
-    grouped = own_query.transpose(1, 0, 2, 3).reshape(rows, kv_heads, per_kv, HEAD_WIDTH)
-    context_dev = cache_keys.shape[1]
-    prior_keys = cache_keys.reshape(rows, context_dev, kv_heads, HEAD_WIDTH)
-    prior_values = cache_values.reshape(rows, context_dev, kv_heads, HEAD_WIDTH)
-    old_scores = (
-        jnp.einsum("bhgd,blhd->bhgl", grouped, prior_keys, preferred_element_type=jnp.float32)
-        * inv_scale
-    )
-    usable = (rank * context_dev + jnp.arange(context_dev, dtype=jnp.int32))[
-        None, :
-    ] < cached_length[:, None]
-    old_scores = jnp.where(usable[:, None, None, :], old_scores, masked_score)
-    old_peak = jnp.max(old_scores, axis=-1)
-    old_weights = jnp.exp(old_scores - old_peak[..., None])
-    old_total = jnp.sum(old_weights, axis=-1)
-    old_sum = jnp.einsum(
-        "bhgl,blhd->bhgd",
-        old_weights.astype(jnp.bfloat16),
-        prior_values,
-        preferred_element_type=jnp.float32,
-    )
-
-    mixed = jnp.einsum(
-        "jtois,tosf->ojif",
-        weights,
-        sorted_x.reshape(ranks, groups, share, features),
+
+    def spread(query):
+        query = query.reshape(-1, heads, 1, HEAD_WIDTH)
+        query = jnp.where(own_kv[None, :, :, None], query, jnp.zeros_like(query))
+        return query.reshape(-1, heads, kv_heads * HEAD_WIDTH)
+
+    weights, fresh_stats, old_all = fresh_weights(
+        ranks,
+        groups,
+        inv_scale,
+        keys,
+        spread(fresh_query).reshape(groups * heads, kv_heads * HEAD_WIDTH),
+        base_cos,
+        base_sin,
+        step_cos,
+        step_sin,
+        owner_of,
+        cache_keys,
+        cache_values,
+        spread(own_query.transpose(1, 0, 2, 3)),
+        jnp.broadcast_to(cached_length[:, None], (rows, HEAD_WIDTH)),
+    )
+
+    weights = weights.transpose(0, 2, 1, 3).reshape(heads, tokens)
+    owned = owner_of.reshape(1, 1, tokens) == jnp.arange(groups, dtype=jnp.int32)[:, None, None]
+    weights = jnp.where(owned, weights[None], jnp.zeros_like(weights)[None])
+    mixed = jnp.dot(
+        weights.reshape(groups * heads, tokens),
+        prefill_states,
         preferred_element_type=jnp.float32,
     )
     fresh_sum = jnp.einsum(
@@ -635,17 +733,6 @@
         preferred_element_type=jnp.float32,
     ).reshape(groups, ranks, local_heads, HEAD_WIDTH)
 
-    about = jnp.concatenate(
-        [old_peak.reshape(rows, heads), old_total.reshape(rows, heads)], axis=0
-    )
-    about = jnp.pad(about.T, ((0, 0), (0, HEAD_WIDTH - 2 * rows)))
-    old_all = jnp.concatenate(
-        [
-            old_sum.reshape(rows, ranks, local_heads, HEAD_WIDTH).transpose(1, 0, 2, 3),
-            about.reshape(ranks, 1, local_heads, HEAD_WIDTH),
-        ],
-        axis=1,
-    )
     result = blend(senders, fresh_sum, fresh_stats, old_all)
     return result.reshape(rows, local_heads * HEAD_WIDTH)
 

time: 108 us -> 89.2 us (0.83)
  Pallas kernels: 76 us -> 63.2 us
  matrix products: 17.6 us -> 11.9 us
    pallas_call x2 -> x1, Pallas kernels: 45.3 us -> 28.5 us  [fresh_weights(): pl.pallas_call(functools.partial(weight_kernel, ranks, owners, scale), in...]
    pallas_call x1, Pallas kernels: 14.2 us -> 20.3 us  [gather_queries(): pl.pallas_call(functools.partial(gather_kernel, groups, ranks, senders),...]
    dot_general x3 -> x1, matrix products: 8.26 us -> 2.38 us  [per_device(): jnp.dot(weights.reshape(groups * heads, tokens), prefill_states, preferre...]
    pallas_call x1, Pallas kernels: 16.5 us -> 14.4 us  [blend(): pl.pallas_call(functools.partial(blend_kernel, groups, ranks, senders), i...]
    unnamed x16 -> x22, local copies, waits for them, and re-layouts: 3.04 us -> 4.99 us
where the time goes in v3:
time: 89.2 us; the launch traced here: 88.9 us
  Pallas kernels  63.2 us (71%)
  matrix products  11.9 us (13%)
  local copies, waits for them, and re-layouts  7.1 us (8%)
  other arithmetic  6.38 us (7%)
    pallas_call x1, Pallas kernels, fresh_weights(): pl.pallas_call(functools.partial(weight_kernel, ranks, owners, scale), in...  28.5 us
    pallas_call x1, Pallas kernels, gather_queries(): pl.pallas_call(functools.partial(gather_kernel, groups, ranks, senders),...  20.3 us
    pallas_call x1, Pallas kernels, blend(): pl.pallas_call(functools.partial(blend_kernel, groups, ranks, senders), i...  14.4 us
    dot_general x1, matrix products, per_device(): jnp.dot(decode_states, query_weight, preferred_element_type=jnp.float32)  8.23 us
    unnamed x22, local copies, waits for them, and re-layouts  4.99 us
    another operation x5, other arithmetic  4.08 us
    dot_general x1, matrix products, per_device(): jnp.dot(weights.reshape(groups * heads, tokens), prefill_states, preferre...  2.38 us

profile of v3, /device:TPU:0, one launch (start us, length us, event | category | flops | bytes accessed | tf_op | source)
XLA Modules:
  0.0 88.9 jit_solution(16184448993434717327)
XLA Ops:
  0.0 0.0 copy-start
  0.0 0.7 compare_reduce_fusion.1
  0.7 0.6 compare_reduce_fusion
  1.3 1.3 %fusion.10 = s32[1,64]{1,0:T(1,128)S(1)} fusion(s32[1,1,64]{2,1,0:T(1,128)} %param.16, pred[]{:T(512)} %compare_reduce_fusion.1), kind=kLoop, calls=%fused_computation.57 | loop fusion | flops 64 | bytes 513 | tf_op jit(solution)/shard_map/reshape.294
  2.7 0.1 pad.19.clone
  2.8 1.3 %fusion.11 = (s32[1,4]{1,0:T(1,128)S(1)}, f32[4]{0:T(128)S(1)}) fusion(s32[4]{0:T(128)} %param.21, pred[]{:T(512)} %compare_reduce_fusion), kind=kLoop, calls=%fused_computation.58 | loop fusion | flops 12 | bytes 49 | tf_op jit(solution)/shard_map/reshape.71
  4.1 0.7 broadcast_in_dim.127.limits
  4.8 0.1 fusion.4.meta
  4.9 0.1 multiply_cosine_fusion.2
  5.0 0.1 iota_compare_fusion.1
  5.1 0.1 multiply_sine_fusion.1
  5.2 0.1 pad_maximum_fusion.3
  5.3 8.2 %convolution_bitcast_fusion = f32[1,4,8,128]{3,1,2,0:T(4,128)S(1)} fusion(bf16[4,8192]{1,0:T(4,128)(2,1)} %param.17, bf16[8192,1024]{1,0:T(8,128)(2,1)} %param.18), kind=kOutput, calls=%fused_computation.6 | convolution fusion | flops 67108864 | bytes 16859136 | tf_op jit(solution)/shard_map/dot_general | solution.py:656
  13.5 0.1 subtract_convert_fusion
  13.6 0.1 pad_maximum_fusion.2.query
  13.7 0.1 broadcast_in_dim.120
  13.9 0.0 slice-done
  13.9 0.3 slice-done.1
  14.2 0.0 copy-done.2
  14.2 20.3 %shard_map.91 = (bf16[8,4,8,128]{3,2,1,0:T(8,128)(2,1)S(1)}, bf16[4,8,8,128]{3,2,1,0:T(8,128)(2,1)S(1)}, s32[8,8,128]{2,1,0:T(8,128)S(1)}, s32[4,8,128]{2,1,0:T(8,128)S(1)}, bf16[4096,1024]{1,0:T(8,128)(2,1)S(1)}) custom-call(bf16[4,8,128]{2,1,0:T(8,128)(2,1)S(1)} %pad_maximum_fusion.2.query, s32[8,128]{1,0:T(8,128)S(1)} %fusion.4.meta, ...), custom_call_target="tpu_custom_call" | custom-call | tf_op jit(solution)/shard_map/pallas_call | solution.py:218
  34.5 0.0 copy-start.1
  34.5 3.2 %copy-done.1 = bf16[4096,1024]{1,0:T(8,128)(2,1)} copy-done((bf16[4096,1024]{1,0:T(8,128)(2,1)}, bf16[4096,1024]{1,0:T(8,128)(2,1)S(1)}, u32[]{:S(2)}) %copy-start.1) | copy-done | bytes 8388632
  37.8 0.1 squeeze.12
  37.8 0.2 dynamic-slice_reduce_fusion
  38.1 0.1 select_reduce_fusion
  38.2 0.1 broadcast_add_fusion
  38.2 0.1 add.75
  38.4 0.1 broadcast_in_dim.112
  38.5 0.2 reshape_reshape.5.owner_of
  38.7 0.1 eq.60
  38.8 0.1 broadcast_in_dim.124
  38.9 0.2 broadcast_in_dim.125
  39.2 0.1 broadcast_select_fusion.2
  39.4 0.1 copy.37
  39.5 1.0 %multiply_sine_fusion = (f32[512,64]{1,0:T(8,128)S(1)}, f32[512,64]{1,0:T(8,128)S(1)}) fusion(f32[64]{0:T(128)S(1)} %multiply_power_fusion, f32[512]{0:T(512)S(1)} %fusion.9), kind=kLoop, calls=%fused_computation.10 | loop fusion | flops 32768 | bytes 264448 | tf_op jit(solution)/shard_map/sin | solution.py:28
  40.4 0.2 pad_maximum_fusion
  40.6 0.0 slice-start.2
  40.7 0.0 slice-start.3
  40.7 28.5 %shard_map.92 = (bf16[8,8,8,512]{3,2,1,0:T(8,128)(2,1)S(1)}, f32[4,8,128]{2,1,0:T(8,128)S(1)}, f32[8,5,8,128]{3,2,1,0:T(8,128)S(1)}) custom-call(bf16[4096,1024]{1,0:T(8,128)(2,1)} %copy-done.1, bf16[256,1024]{1,0:T(8,128)(2,1)S(1)} %bitcast.61, f32[512,128]{1,0:T(8,128)S(1)} %get-tuple-element.57.base_cos, f32[512,128]{1,0:T(8,128)S(1)} %get-tuple-element.58.base_sin, ...), custom_call_target="tpu_custom_call" | custom-call | tf_op jit(solution)/shard_map/pallas_call | solution.py:479
  69.2 0.0 copy-start.3
  69.2 0.2 broadcast_select_fusion
  69.4 2.4 %convolution_convert_fusion = bf16[256,1024]{1,0:T(8,128)(2,1)S(1)} fusion(bf16[256,4096]{1,0:T(8,128)(2,1)S(1)} %bitcast.64, bf16[4096,1024]{1,0:T(8,128)(2,1)S(1)} %bitcast.60), kind=kOutput, calls=%fused_computation.4 | convolution fusion | flops 2147745792 | bytes 11010048 | tf_op jit(solution)/shard_map/dot_general | solution.py:724
  71.8 0.0 copy-done.3
  71.8 0.0 copy-done.4
  71.9 0.0 copy-done
  71.9 1.3 %fusion.2.fresh = f32[4,8,8,128]{3,2,1,0:T(8,128)} fusion(bf16[4,8,8,1024]{3,2,1,0:T(8,128)(2,1)S(1)} %bitcast.66, bf16[1024,1024]{1,0:T(8,128)(2,1)S(1)} %copy-done), kind=kOutput, calls=%fused_computation.5 | convolution fusion | flops 67108864 | bytes 2752512 | tf_op jit(solution)/shard_map/oknf,fkd->oknd/dot_general | solution.py:729
  73.1 14.4 %shard_map.93 = bf16[4,8,128]{2,1,0:T(8,128)(2,1)} custom-call(f32[4,8,8,128]{3,2,1,0:T(8,128)} %fusion.2.fresh, f32[4,8,128]{2,1,0:T(8,128)} %copy-done.4, f32[8,5,8,128]{3,2,1,0:T(8,128)} %copy-done.3), custom_call_target="tpu_custom_call" | custom-call | tf_op jit(solution)/shard_map/pallas_call | solution.py:612
  87.6 1.3 %copy.40 = bf16[1,4,8,128]{3,1,2,0:T(4,128)(2,1)} copy(bf16[1,4,8,128]{3,2,1,0:T(8,128)(2,1)} %bitcast.70) | data formatting | bytes 16384
  (22 shorter events, 0.2 us)
Async XLA Ops:
  0.0 71.9 %copy-start = (bf16[1024,1024]{1,0:T(8,128)(2,1)S(1)}, bf16[1024,1024]{1,0:T(8,128)(2,1)}, u32[]{:S(2)}) copy-start(bf16[1024,1024]{1,0:T(8,128)(2,1)} %param.15) | copy-start | bytes 6291460
  5.3 8.6 %slice-start = ((s8[8388608]{0:T(1024)(128)(4,1)}), s8[4194304]{0:T(1024)(128)(4,1)S(1)}, s32[]{:S(2)}) async-start(s8[8388608]{0:T(1024)(128)(4,1)} %bitcast.57), calls=%async_computation | async-start | bytes 8388608
  5.3 8.9 %slice-start.1 = ((s8[8388608]{0:T(1024)(128)(4,1)}), s8[4194304]{0:T(1024)(128)(4,1)S(1)}, s32[]{:S(2)}) async-start(s8[8388608]{0:T(1024)(128)(4,1)} %bitcast.57), calls=%async_computation.1 | async-start | bytes 8388608
  5.3 8.9 %copy-start.2 = (bf16[1024,1024]{1,0:T(8,128)(2,1)S(1)}, bf16[1024,1024]{1,0:T(8,128)(2,1)}, u32[]{:S(2)}) copy-start(bf16[1024,1024]{1,0:T(8,128)(2,1)} %weight.1) | copy-start | bytes 6291460
  34.5 3.2 %copy-start.1 = (bf16[4096,1024]{1,0:T(8,128)(2,1)}, bf16[4096,1024]{1,0:T(8,128)(2,1)S(1)}, u32[]{:S(2)}) copy-start(bf16[4096,1024]{1,0:T(8,128)(2,1)S(1)} %get-tuple-element.38.keys) | copy-start | bytes 25165828
  40.6 28.8 %slice-start.2 = ((s8[8388608]{0:T(1024)(128)(4,1)}), s8[4194304]{0:T(1024)(128)(4,1)S(1)}, s32[]{:S(2)}) async-start(s8[8388608]{0:T(1024)(128)(4,1)} %bitcast.59), calls=%async_computation.2 | async-start | bytes 8388608
  40.7 28.8 %slice-start.3 = ((s8[8388608]{0:T(1024)(128)(4,1)}), s8[4194304]{0:T(1024)(128)(4,1)S(1)}, s32[]{:S(2)}) async-start(s8[8388608]{0:T(1024)(128)(4,1)} %bitcast.59), calls=%async_computation.3 | async-start | bytes 8388608
  69.2 2.6 %copy-start.3 = (f32[8,5,8,128]{3,2,1,0:T(8,128)}, f32[8,5,8,128]{3,2,1,0:T(8,128)S(1)}, u32[]{:S(2)}) copy-start(f32[8,5,8,128]{3,2,1,0:T(8,128)S(1)} %get-tuple-element.44.old) | copy-start | bytes 491524
  69.2 2.6 %copy-start.4 = (f32[4,8,128]{2,1,0:T(8,128)}, f32[4,8,128]{2,1,0:T(8,128)S(1)}, u32[]{:S(2)}) copy-start(f32[4,8,128]{2,1,0:T(8,128)S(1)} %get-tuple-element.43.stats) | copy-start | bytes 49156

commit v4 on v3

--- a/solution.py
+++ b/solution.py
@@ -218,7 +218,7 @@
     return pl.pallas_call(
         functools.partial(gather_kernel, groups, ranks, senders),
         in_specs=[vmem, vmem, hbm, vmem],
-        out_specs=[vmem] * 4 + [hbm],
+        out_specs=[vmem] * 4 + [pl.BlockSpec(memory_space=pl.ANY)],
         out_shape=[
             jax.ShapeDtypeStruct((ranks, rows, local_heads, width), query.dtype),
             jax.ShapeDtypeStruct((groups, ranks, local_heads, width), query.dtype),
@@ -234,7 +234,7 @@
             dma((2,)), dma((2,)),
         ],
         compiler_params=pltpu.CompilerParams(
-            collective_id=0, has_side_effects=True, vmem_limit_bytes=32 * 1024 * 1024
+            collective_id=0, has_side_effects=True, vmem_limit_bytes=60 * 1024 * 1024
         ),
     )(query, meta, states, weight)
 
@@ -243,8 +243,9 @@
     ranks, owners, scale, keys, queries, base_cos, base_sin, step_cos, step_sin, owner_of,
     cache_keys, cache_values, own_queries, limits,
     weights, stats, old,
-    partial_scores, paired, chip_sums, incoming, key_tiles, turned, old_keys, old_values,
+    partial_scores, paired, chip_sums, incoming, key_tiles, turned, old_keys, old_values, old_own,
     send_pair, send_sum, send_weight, send_on, got_pair, got_sum, got_weight, key_sems, old_sems,
+    send_old, got_old,
 ):
     group, rank = lax.axis_index("group"), lax.axis_index("tensor")
     chips = ranks // 2
@@ -271,7 +272,7 @@
         other = lax.rem(chip + step, chips)
         return other, other * 2 + core
 
-    for peer in [partner] + [peer_of(step)[1] for step in range(1, chips)]:
+    for peer in [lax.rem(rank + step, ranks) for step in range(1, ranks)]:
         pl.semaphore_signal(
             barrier,
             inc=1,
@@ -280,7 +281,7 @@
         )
     key_old = pltpu.make_async_copy(cache_keys, old_keys, old_sems.at[0])
     value_old = pltpu.make_async_copy(cache_values, old_values, old_sems.at[1])
-    pl.semaphore_wait(barrier, chips)
+    pl.semaphore_wait(barrier, ranks - 1)
 
     def pair_copy(block):
         return remote(
@@ -382,11 +383,21 @@
         about = jnp.where(lane == b, old_peak, jnp.where(lane == rows + b, old_total, about))
         for j in range(ranks):
             h = j * local_heads // per_kv
-            old[j, b] = old_sum[
+            old_own[j, b] = old_sum[
                 j * local_heads : (j + 1) * local_heads, h * HEAD_WIDTH : (h + 1) * HEAD_WIDTH
             ]
     for j in range(ranks):
-        old[j, rows] = about[j * local_heads : (j + 1) * local_heads]
+        old_own[j, rows] = about[j * local_heads : (j + 1) * local_heads]
+
+    def old_copy(step):
+        peer = lax.rem(rank + step, ranks)
+        return remote(
+            old_own.at[peer], old.at[rank], send_old.at[step], got_old.at[rank], group, peer
+        )
+
+    for step in range(1, ranks):
+        old_copy(step).start()
+    old[rank] = old_own[rank]
 
     for step in range(1, chips):
         other, peer = peer_of(step)
@@ -457,6 +468,12 @@
         return carry
 
     lax.fori_loop(0, ranks, sent, 0)
+    for step in range(1, ranks):
+        source = lax.rem(rank + step, ranks)
+        remote(
+            old_own.at[source], old.at[source], send_old.at[step], got_old.at[source], group, source
+        ).wait_recv()
+        old_copy(step).wait_send()
     for step in range(chips):
         on_copy(step).wait_send()
         if step:
@@ -478,7 +495,7 @@
     held = (chips, local_heads, tile)
     return pl.pallas_call(
         functools.partial(weight_kernel, ranks, owners, scale),
-        in_specs=[hbm] + [vmem] * 6 + [hbm] * 2 + [vmem] * 2,
+        in_specs=[pl.BlockSpec(memory_space=pl.ANY)] + [vmem] * 6 + [hbm] * 2 + [vmem] * 2,
         out_specs=[vmem] * 3,
         out_shape=[
             jax.ShapeDtypeStruct((ranks, ranks, local_heads, tile), jnp.bfloat16),
@@ -494,11 +511,13 @@
             pltpu.VMEM((tile, width), jnp.bfloat16),
             pltpu.VMEM(cache_keys.shape, jnp.bfloat16),
             pltpu.VMEM(cache_values.shape, jnp.bfloat16),
+            pltpu.VMEM((ranks, rows + 1, local_heads, HEAD_WIDTH), jnp.float32),
             dma((ranks,)), dma((chips, ranks)), dma((chips,)), dma((chips,)),
             dma((ranks,)), dma((chips, ranks)), dma((ranks,)), dma((2,)), dma((2,)),
+            dma((ranks,)), dma((ranks,)),
         ],
         compiler_params=pltpu.CompilerParams(
-            collective_id=1, has_side_effects=True, vmem_limit_bytes=48 * 1024 * 1024
+            collective_id=1, has_side_effects=True, vmem_limit_bytes=28 * 1024 * 1024
         ),
     )(
         keys, queries, base_cos, base_sin, step_cos, step_sin, owner_of,
@@ -507,8 +526,8 @@
 
 
 def blend_kernel(
-    groups, ranks, senders, fresh, stats, old, out, fresh_in, stats_in, old_in,
-    send_fresh, send_stats, send_old, got_fresh, got_stats, got_old,
+    groups, ranks, senders, fresh, stats, old_in, out, fresh_in, stats_in,
+    send_fresh, send_stats, got_fresh, got_stats,
 ):
     group, rank = lax.axis_index("group"), lax.axis_index("tensor")
     rows = out.shape[0]
@@ -537,14 +556,6 @@
             stats.at[peer], stats_in.at[group], send_stats.at[step], got_stats.at[group], peer, rank
         )
 
-    def old_copy(step):
-        peer = lax.rem(rank + step, ranks)
-        return remote(
-            old.at[peer], old_in.at[rank], send_old.at[step], got_old.at[rank], group, peer
-        )
-
-    for step in range(1, ranks):
-        old_copy(step).start()
     for step in range(1, groups):
         stats_copy(step).start()
 
@@ -553,14 +564,8 @@
         return carry
 
     lax.fori_loop(1, count, start, 0)
-    old_in[rank] = old[rank]
     stats_in[group] = stats[group]
     fresh_in[group, rank] = fresh[group, rank]
-    for step in range(1, ranks):
-        source = lax.rem(rank + step, ranks)
-        remote(
-            old.at[source], old_in.at[source], send_old.at[step], got_old.at[source], group, source
-        ).wait_recv()
     for step in range(1, groups):
         source = lax.rem(group + step, groups)
         remote(
@@ -598,8 +603,6 @@
         numerator = sum(a * b for a, b in zip(sums, factors))
         denominator = sum(a * b for a, b in zip(totals, factors))
         out[row] = (numerator / denominator).astype(out.dtype)
-    for step in range(1, ranks):
-        old_copy(step).wait_send()
     for step in range(1, groups):
         stats_copy(step).wait_send()
 
@@ -617,9 +620,7 @@
         scratch_shapes=[
             pltpu.VMEM(fresh.shape, jnp.float32),
             pltpu.VMEM(stats.shape, jnp.float32),
-            pltpu.VMEM(old.shape, jnp.float32),
-            dma((groups * ranks,)), dma((groups,)), dma((ranks,)),
-            dma((groups, ranks)), dma((groups,)), dma((ranks,)),
+            dma((groups * ranks,)), dma((groups,)), dma((groups, ranks)), dma((groups,)),
         ],
         compiler_params=pltpu.CompilerParams(collective_id=2, has_side_effects=True),
     )(fresh, stats, old)

time: 89.2 us -> 98.3 us (1.10)
  local copies, waits for them, and re-layouts: 7.1 us -> 12.1 us
  matrix products: 11.9 us -> 15.1 us
  other arithmetic: 6.38 us -> 7.51 us
    dot_general x1, matrix products: 2.38 us -> 5.76 us  [per_device(): jnp.dot(weights.reshape(groups * heads, tokens), prefill_states, preferre...]
    pallas_call x1, Pallas kernels: 14.4 us -> 11.1 us  [blend(): pl.pallas_call(functools.partial(blend_kernel, groups, ranks, senders), i...]
    pallas_call x1, Pallas kernels: 20.3 us -> 23.4 us  [gather_queries(): pl.pallas_call(functools.partial(gather_kernel, groups, ranks, senders),...]
    unnamed x22 -> x18, local copies, waits for them, and re-layouts: 4.99 us -> 7.69 us
where the time goes in v4:
time: 98.3 us; the launch traced here: 97.5 us
  Pallas kernels  62.5 us (64%)
  matrix products  15.1 us (15%)
  local copies, waits for them, and re-layouts  12.1 us (12%)
  other arithmetic  7.51 us (8%)
    pallas_call x1, Pallas kernels, fresh_weights(): pl.pallas_call(functools.partial(weight_kernel, ranks, owners, scale), in...  28 us
    pallas_call x1, Pallas kernels, gather_queries(): pl.pallas_call(functools.partial(gather_kernel, groups, ranks, senders),...  23.4 us
    pallas_call x1, Pallas kernels, blend(): pl.pallas_call(functools.partial(blend_kernel, groups, ranks, senders), i...  11.1 us
    dot_general x1, matrix products, per_device(): jnp.dot(decode_states, query_weight, preferred_element_type=jnp.float32)  8.08 us
    unnamed x18, local copies, waits for them, and re-layouts  7.69 us
    dot_general x1, matrix products, per_device(): jnp.dot(weights.reshape(groups * heads, tokens), prefill_states, preferre...  5.76 us
    another operation x5, other arithmetic  4.02 us

profile of v4, /device:TPU:0, one launch (start us, length us, event | category | flops | bytes accessed | tf_op | source)
XLA Modules:
  0.0 97.5 jit_solution(12072990576156594374)
XLA Ops:
  0.0 0.0 copy-start
  0.0 0.7 compare_reduce_fusion.1
  0.7 0.6 compare_reduce_fusion
  1.3 1.3 %fusion.10 = s32[1,64]{1,0:T(1,128)S(1)} fusion(s32[1,1,64]{2,1,0:T(1,128)} %param.16, pred[]{:T(512)} %compare_reduce_fusion.1), kind=kLoop, calls=%fused_computation.57 | loop fusion | flops 64 | bytes 513 | tf_op jit(solution)/shard_map/reshape.294
  2.7 0.1 pad.19.clone
  2.7 1.3 %fusion.11 = (s32[1,4]{1,0:T(1,128)S(1)}, f32[4]{0:T(128)S(1)}) fusion(s32[4]{0:T(128)} %param.21, pred[]{:T(512)} %compare_reduce_fusion), kind=kLoop, calls=%fused_computation.58 | loop fusion | flops 12 | bytes 49 | tf_op jit(solution)/shard_map/reshape.71
  4.0 0.7 broadcast_in_dim.127.limits
  4.8 0.7 fusion.4.meta
  5.4 0.1 multiply_cosine_fusion.2
  5.5 0.1 iota_compare_fusion.1
  5.6 0.1 multiply_sine_fusion.1
  5.7 0.1 pad_maximum_fusion.3
  5.8 8.1 %convolution_bitcast_fusion = f32[1,4,8,128]{3,1,2,0:T(4,128)S(1)} fusion(bf16[4,8192]{1,0:T(4,128)(2,1)} %param.17, bf16[8192,1024]{1,0:T(8,128)(2,1)} %param.18), kind=kOutput, calls=%fused_computation.6 | convolution fusion | flops 67108864 | bytes 16859136 | tf_op jit(solution)/shard_map/dot_general | solution.py:657
  13.9 0.1 subtract_convert_fusion
  14.0 0.7 pad_maximum_fusion.2.query
  14.7 0.1 broadcast_in_dim.120
  14.8 23.4 %shard_map.91 = (bf16[8,4,8,128]{3,2,1,0:T(8,128)(2,1)}, bf16[4,8,8,128]{3,2,1,0:T(8,128)(2,1)}, s32[8,8,128]{2,1,0:T(8,128)}, s32[4,8,128]{2,1,0:T(8,128)}, bf16[4096,1024]{1,0:T(8,128)(2,1)}) custom-call(bf16[4,8,128]{2,1,0:T(8,128)(2,1)} %pad_maximum_fusion.2.query, s32[8,128]{1,0:T(8,128)} %fusion.4.meta, bf16[4096,1024]{1,0:T(8,128)(2,1)} %states.1, ...), custom_call_target="tpu_custom_call" | custom-call | tf_op jit(solution)/shard_map/pallas_call | solution.py:218
  38.3 0.0 copy-start.6
  38.3 0.8 slice_reduce_fusion
  39.1 0.1 squeeze.12
  39.2 0.7 slice.47
  39.9 0.2 dynamic-slice_reduce_fusion
  40.1 0.1 select_reduce_fusion
  40.2 0.1 broadcast_add_fusion
  40.3 0.1 add.75
  40.4 0.9 copy_bitcast_fusion.2
  41.3 0.1 broadcast_in_dim.112
  41.4 0.2 reshape_reshape.5.owner_of
  41.6 0.1 eq.60
  41.7 0.1 broadcast_in_dim.124
  41.8 0.2 broadcast_in_dim.125
  42.1 0.0 copy-start.2
  42.1 0.0 copy-done.6
  42.1 0.1 broadcast_select_fusion.2
  42.3 0.1 copy.37
  42.4 1.0 %multiply_sine_fusion = (f32[512,64]{1,0:T(8,128)S(1)}, f32[512,64]{1,0:T(8,128)S(1)}) fusion(f32[64]{0:T(128)S(1)} %multiply_power_fusion, f32[512]{0:T(512)S(1)} %fusion.9), kind=kLoop, calls=%fused_computation.10 | loop fusion | flops 32768 | bytes 264448 | tf_op jit(solution)/shard_map/sin | solution.py:28
  43.4 0.2 pad_maximum_fusion
  43.6 0.7 copy-done.2
  44.2 3.4 %copy-done.1 = bf16[4096,1024]{1,0:T(8,128)(2,1)S(1)} copy-done((bf16[4096,1024]{1,0:T(8,128)(2,1)S(1)}, bf16[4096,1024]{1,0:T(8,128)(2,1)}, u32[]{:S(2)}) %copy-start.1) | copy-done | bytes 8388632
  47.6 2.2 %copy-done.3 = bf16[4,512,1024]{2,1,0:T(8,128)(2,1)S(1)} copy-done((bf16[4,512,1024]{2,1,0:T(8,128)(2,1)S(1)}, bf16[4,512,1024]{2,1,0:T(8,128)(2,1)}, u32[]{:S(2)}) %copy-start.3) | copy-done | bytes 4194328
  49.8 28.0 %shard_map.92 = (bf16[8,8,8,512]{3,2,1,0:T(8,128)(2,1)S(1)}, f32[4,8,128]{2,1,0:T(8,128)S(1)}, f32[8,5,8,128]{3,2,1,0:T(8,128)S(1)}) custom-call(bf16[4096,1024]{1,0:T(8,128)(2,1)S(1)} %copy-done.1, bf16[256,1024]{1,0:T(8,128)(2,1)S(1)} %bitcast.57, f32[512,128]{1,0:T(8,128)S(1)} %get-tuple-element.57.base_cos, f32[512,128]{1,0:T(8,128)S(1)} %get-tuple-element.58.base_sin, ...), custom_call_target="tpu_custom_call" | custom-call | tf_op jit(solution)/shard_map/pallas_call | solution.py:496
  77.8 0.0 copy-start.4
  77.8 0.0 copy-start.5
  77.8 0.2 broadcast_select_fusion
  78.1 5.8 %convolution_convert_fusion = bf16[256,1024]{1,0:T(8,128)(2,1)S(1)} fusion(bf16[256,4096]{1,0:T(8,128)(2,1)S(1)} %bitcast.59, bf16[4096,1024]{1,0:T(8,128)(2,1)} %states.1), kind=kOutput, calls=%fused_computation.4 | convolution fusion | flops 2147745792 | bytes 11010048 | tf_op jit(solution)/shard_map/dot_general | solution.py:725
  83.9 1.3 %fusion.2.fresh = f32[4,8,8,128]{3,2,1,0:T(8,128)} fusion(bf16[4,8,8,1024]{3,2,1,0:T(8,128)(2,1)S(1)} %bitcast.61, bf16[1024,1024]{1,0:T(8,128)(2,1)S(1)} %copy-done), kind=kOutput, calls=%fused_computation.5 | convolution fusion | flops 67108864 | bytes 2752512 | tf_op jit(solution)/shard_map/oknf,fkd->oknd/dot_general | solution.py:730
  85.1 11.1 %shard_map.93 = bf16[4,8,128]{2,1,0:T(8,128)(2,1)} custom-call(f32[4,8,8,128]{3,2,1,0:T(8,128)} %fusion.2.fresh, f32[4,8,128]{2,1,0:T(8,128)} %copy-done.5, f32[8,5,8,128]{3,2,1,0:T(8,128)} %copy-done.4), custom_call_target="tpu_custom_call" | custom-call | tf_op jit(solution)/shard_map/pallas_call | solution.py:615
  96.2 1.3 %copy.40 = bf16[1,4,8,128]{3,1,2,0:T(4,128)(2,1)} copy(bf16[1,4,8,128]{3,2,1,0:T(8,128)(2,1)} %bitcast.66) | data formatting | bytes 16384
  (16 shorter events, 0.2 us)
Async XLA Ops:
  0.0 83.8 %copy-start = (bf16[1024,1024]{1,0:T(8,128)(2,1)S(1)}, bf16[1024,1024]{1,0:T(8,128)(2,1)}, u32[]{:S(2)}) copy-start(bf16[1024,1024]{1,0:T(8,128)(2,1)} %param.15) | copy-start | bytes 6291460
  38.3 3.8 %copy-start.6 = (bf16[4,8,8,128]{3,2,1,0:T(8,128)(2,1)S(1)}, bf16[4,8,8,128]{3,2,1,0:T(8,128)(2,1)}, u32[]{:S(2)}) copy-start(bf16[4,8,8,128]{3,2,1,0:T(8,128)(2,1)} %get-tuple-element.39) | copy-start | bytes 196612
  42.1 2.2 %copy-start.2 = (bf16[4,512,1024]{2,1,0:T(8,128)(2,1)S(1)}, bf16[4,512,1024]{2,1,0:T(8,128)(2,1)}, u32[]{:S(2)}) copy-start(bf16[4,512,1024]{2,1,0:T(8,128)(2,1)} %cache_keys.1) | copy-start | bytes 12582916
  44.2 3.4 %copy-start.1 = (bf16[4096,1024]{1,0:T(8,128)(2,1)S(1)}, bf16[4096,1024]{1,0:T(8,128)(2,1)}, u32[]{:S(2)}) copy-start(bf16[4096,1024]{1,0:T(8,128)(2,1)} %get-tuple-element.38.keys) | copy-start | bytes 25165828
  47.6 2.2 %copy-start.3 = (bf16[4,512,1024]{2,1,0:T(8,128)(2,1)S(1)}, bf16[4,512,1024]{2,1,0:T(8,128)(2,1)}, u32[]{:S(2)}) copy-start(bf16[4,512,1024]{2,1,0:T(8,128)(2,1)} %cache_values.1) | copy-start | bytes 12582916
  77.8 6.0 %copy-start.4 = (f32[8,5,8,128]{3,2,1,0:T(8,128)}, f32[8,5,8,128]{3,2,1,0:T(8,128)S(1)}, u32[]{:S(2)}) copy-start(f32[8,5,8,128]{3,2,1,0:T(8,128)S(1)} %get-tuple-element.44.old_in) | copy-start | bytes 491524
  77.8 6.0 %copy-start.5 = (f32[4,8,128]{2,1,0:T(8,128)}, f32[4,8,128]{2,1,0:T(8,128)S(1)}, u32[]{:S(2)}) copy-start(f32[4,8,128]{2,1,0:T(8,128)S(1)} %get-tuple-element.43.stats) | copy-start | bytes 49156

commit v5 on v4

--- a/solution.py
+++ b/solution.py
@@ -495,7 +495,7 @@
     held = (chips, local_heads, tile)
     return pl.pallas_call(
         functools.partial(weight_kernel, ranks, owners, scale),
-        in_specs=[pl.BlockSpec(memory_space=pl.ANY)] + [vmem] * 6 + [hbm] * 2 + [vmem] * 2,
+        in_specs=[hbm] + [vmem] * 6 + [hbm] * 2 + [vmem] * 2,
         out_specs=[vmem] * 3,
         out_shape=[
             jax.ShapeDtypeStruct((ranks, ranks, local_heads, tile), jnp.bfloat16),
@@ -517,7 +517,7 @@
             dma((ranks,)), dma((ranks,)),
         ],
         compiler_params=pltpu.CompilerParams(
-            collective_id=1, has_side_effects=True, vmem_limit_bytes=28 * 1024 * 1024
+            collective_id=1, has_side_effects=True, vmem_limit_bytes=60 * 1024 * 1024
         ),
     )(
         keys, queries, base_cos, base_sin, step_cos, step_sin, owner_of,

time: 98.3 us -> 101 us (1.027)
  local copies, waits for them, and re-layouts: 12.1 us -> 7.9 us
  Pallas kernels: 62.5 us -> 65.9 us
  other arithmetic: 7.51 us -> 10.9 us
    unnamed x18 -> x8, local copies, waits for them, and re-layouts: 7.69 us -> 2.32 us
    pallas_call x1, Pallas kernels: 28 us -> 31.6 us  [fresh_weights(): pl.pallas_call(functools.partial(weight_kernel, ranks, owners, scale), in...]
    concatenate x2, other arithmetic: 0.28 us -> 1.68 us  [full_tables(): jnp.concatenate([cosine_part, cosine_part], axis=-1)]
    select_n x1, other arithmetic: 0.2 us -> 1.24 us  [per_device(): weights = jnp.where(owned, weights[None], jnp.zeros_like(weights)[None])]
where the time goes in v5:
time: 101 us; the launch traced here: 99.9 us
  Pallas kernels  65.9 us (65%)
  matrix products  15.1 us (15%)
  other arithmetic  10.9 us (11%)
  local copies, waits for them, and re-layouts  7.9 us (8%)
    pallas_call x1, Pallas kernels, fresh_weights(): pl.pallas_call(functools.partial(weight_kernel, ranks, owners, scale), in...  31.6 us
    pallas_call x1, Pallas kernels, gather_queries(): pl.pallas_call(functools.partial(gather_kernel, groups, ranks, senders),...  23.4 us
    pallas_call x1, Pallas kernels, blend(): pl.pallas_call(functools.partial(blend_kernel, groups, ranks, senders), i...  10.9 us
    dot_general x1, matrix products, per_device(): jnp.dot(decode_states, query_weight, preferred_element_type=jnp.float32)  8.07 us
    dot_general x1, matrix products, per_device(): jnp.dot(weights.reshape(groups * heads, tokens), prefill_states, preferre...  5.77 us
    another operation x5, other arithmetic  4.1 us
    unnamed x8, local copies, waits for them, and re-layouts  2.32 us

profile of v5, /device:TPU:0, one launch (start us, length us, event | category | flops | bytes accessed | tf_op | source)
XLA Modules:
  0.0 99.9 jit_solution(3775767796073471425)
XLA Ops:
  0.0 0.0 copy-start
  0.0 0.7 compare_reduce_fusion.1
  0.7 0.6 compare_reduce_fusion
  1.4 1.4 %fusion.10 = s32[1,64]{1,0:T(1,128)S(1)} fusion(s32[1,1,64]{2,1,0:T(1,128)} %param.16, pred[]{:T(512)} %compare_reduce_fusion.1), kind=kLoop, calls=%fused_computation.57 | loop fusion | flops 64 | bytes 513 | tf_op jit(solution)/shard_map/reshape.294
  2.7 0.1 pad.19.clone
  2.8 1.3 %fusion.11 = (s32[1,4]{1,0:T(1,128)S(1)}, f32[4]{0:T(128)S(1)}) fusion(s32[4]{0:T(128)} %param.21, pred[]{:T(512)} %compare_reduce_fusion), kind=kLoop, calls=%fused_computation.58 | loop fusion | flops 12 | bytes 49 | tf_op jit(solution)/shard_map/reshape.71
  4.1 1.3 %broadcast_in_dim.127.limits = s32[4,128]{1,0:T(4,128)} broadcast(s32[4]{0:T(128)} %param.21), dimensions={0} | broadcast | bytes 2064 | tf_op jit(solution)/shard_map/broadcast_in_dim | solution.py:719
  5.4 0.7 fusion.4.meta
  6.0 0.1 multiply_cosine_fusion.2
  6.1 0.1 iota_compare_fusion.1
  6.2 0.1 multiply_sine_fusion.1
  6.3 0.7 pad_maximum_fusion.3
  7.0 8.1 %convolution_bitcast_fusion = f32[1,4,8,128]{3,1,2,0:T(4,128)S(1)} fusion(bf16[4,8192]{1,0:T(4,128)(2,1)} %param.17, bf16[8192,1024]{1,0:T(8,128)(2,1)} %param.18), kind=kOutput, calls=%fused_computation.6 | convolution fusion | flops 67108864 | bytes 16859136 | tf_op jit(solution)/shard_map/dot_general | solution.py:657
  15.1 0.1 subtract_convert_fusion
  15.2 0.7 pad_maximum_fusion.2.query
  15.9 0.1 broadcast_in_dim.120
  16.0 23.4 %shard_map.91 = (bf16[8,4,8,128]{3,2,1,0:T(8,128)(2,1)}, bf16[4,8,8,128]{3,2,1,0:T(8,128)(2,1)}, s32[8,8,128]{2,1,0:T(8,128)}, s32[4,8,128]{2,1,0:T(8,128)}, bf16[4096,1024]{1,0:T(8,128)(2,1)}) custom-call(bf16[4,8,128]{2,1,0:T(8,128)(2,1)} %pad_maximum_fusion.2.query, s32[8,128]{1,0:T(8,128)} %fusion.4.meta, bf16[4096,1024]{1,0:T(8,128)(2,1)} %states.1, ...), custom_call_target="tpu_custom_call" | custom-call | tf_op jit(solution)/shard_map/pallas_call | solution.py:218
  39.4 0.0 copy-start.1
  39.4 0.8 slice_reduce_fusion
  40.2 0.1 squeeze.12
  40.3 0.7 slice.47
  41.1 0.2 dynamic-slice_reduce_fusion
  41.3 0.1 select_reduce_fusion
  41.4 0.1 broadcast_add_fusion
  41.4 0.1 add.75
  41.5 0.9 copy_bitcast_fusion.2
  42.4 0.1 broadcast_in_dim.112
  42.5 0.8 reshape_reshape.5.owner_of
  43.3 0.1 eq.60
  43.5 0.1 broadcast_in_dim.124
  43.6 0.2 broadcast_in_dim.125
  43.8 0.9 broadcast_select_fusion.1.own_queries
  44.7 0.0 copy-done.1
  44.7 0.1 broadcast_select_fusion.2
  44.8 1.0 copy.37
  45.8 1.0 multiply_sine_fusion
  46.8 1.0 pad_maximum_fusion
  47.8 31.6 %shard_map.92 = (bf16[8,8,8,512]{3,2,1,0:T(8,128)(2,1)}, f32[4,8,128]{2,1,0:T(8,128)}, f32[8,5,8,128]{3,2,1,0:T(8,128)}) custom-call(bf16[4096,1024]{1,0:T(8,128)(2,1)} %get-tuple-element.38.keys, bf16[256,1024]{1,0:T(8,128)(2,1)} %bitcast.58, f32[512,128]{1,0:T(8,128)} %get-tuple-element.57.base_cos, f32[512,128]{1,0:T(8,128)} %get-tuple-element.58.base_sin, ...), custom_call_target="tpu_custom_call" | custom-call | tf_op jit(solution)/shard_map/pallas_call | solution.py:496
  79.4 1.2 %broadcast_select_fusion = bf16[4,64,4096]{2,1,0:T(8,128)(2,1)S(1)} fusion(pred[4,4096]{1,0:T(4,128)(4,1)S(1)} %iota_compare_fusion, bf16[64,4096]{1,0:T(8,128)(2,1)} %bitcast.60), kind=kLoop, calls=%fused_computation.3 | loop fusion | flops 1048576 | bytes 2637824 | tf_op jit(solution)/shard_map/jit(_where)/select_n | solution.py:724
  80.6 5.8 %convolution_convert_fusion = bf16[256,1024]{1,0:T(8,128)(2,1)S(1)} fusion(bf16[256,4096]{1,0:T(8,128)(2,1)S(1)} %bitcast.57, bf16[4096,1024]{1,0:T(8,128)(2,1)} %states.1), kind=kOutput, calls=%fused_computation.4 | convolution fusion | flops 2147745792 | bytes 11010048 | tf_op jit(solution)/shard_map/dot_general | solution.py:725
  86.4 0.0 copy-done
  86.4 1.2 %fusion.2.fresh = f32[4,8,8,128]{3,2,1,0:T(8,128)} fusion(bf16[4,8,8,1024]{3,2,1,0:T(8,128)(2,1)S(1)} %bitcast.61, bf16[1024,1024]{1,0:T(8,128)(2,1)S(1)} %copy-done), kind=kOutput, calls=%fused_computation.5 | convolution fusion | flops 67108864 | bytes 2752512 | tf_op jit(solution)/shard_map/oknf,fkd->oknd/dot_general | solution.py:730
  87.7 10.9 %shard_map.93 = bf16[4,8,128]{2,1,0:T(8,128)(2,1)} custom-call(f32[4,8,8,128]{3,2,1,0:T(8,128)} %fusion.2.fresh, f32[4,8,128]{2,1,0:T(8,128)} %get-tuple-element.43.stats, f32[8,5,8,128]{3,2,1,0:T(8,128)} %get-tuple-element.44.old_in), custom_call_target="tpu_custom_call" | custom-call | tf_op jit(solution)/shard_map/pallas_call | solution.py:615
  98.6 1.3 %copy.40 = bf16[1,4,8,128]{3,1,2,0:T(4,128)(2,1)} copy(bf16[1,4,8,128]{3,2,1,0:T(8,128)(2,1)} %bitcast.66) | data formatting | bytes 16384
  (10 shorter events, 0.1 us)
Async XLA Ops:
  0.0 86.4 %copy-start = (bf16[1024,1024]{1,0:T(8,128)(2,1)S(1)}, bf16[1024,1024]{1,0:T(8,128)(2,1)}, u32[]{:S(2)}) copy-start(bf16[1024,1024]{1,0:T(8,128)(2,1)} %param.15) | copy-start | bytes 6291460
  39.4 5.3 %copy-start.1 = (bf16[4,8,8,128]{3,2,1,0:T(8,128)(2,1)S(1)}, bf16[4,8,8,128]{3,2,1,0:T(8,128)(2,1)}, u32[]{:S(2)}) copy-start(bf16[4,8,8,128]{3,2,1,0:T(8,128)(2,1)} %get-tuple-element.39) | copy-start | bytes 196612
